TPU v7x, 128 devices: a whole 4x4x4 slice. The times are simulated.
128 devices in a mesh: gx: 8 (over x, core), gy: 16 (over y, z).
Axes of the slice: x: 4, y: 4, z: 4, core: 2. Of those that a mesh axis runs over, the one named last changes fastest.
Arguments:
- particles: float32 [16, 1048576], P(None, ('gx', 'gy')), may hold values from -10 to 10
- migrant_index: int32 [512, 512], P(('gx', 'gy')), may hold values from 0 to 8191, as said below
- migrant_count: int32 [128, 4], P(('gx', 'gy')), may hold values from 170 to 512, as said below
- migrated_slot_cell: int32 [1310720], P(('gx', 'gy')), may hold values from 0 to 12287
- source_tile_size: int32 [128, 256], P(('gx', 'gy')), may hold values from 1 to 64, 12288 in all within a row
- tile_owner: int32 [32768, 1], P(('gx', 'gy')), may hold values from 0 to 127; in each aligned block of 256 rows (0 to 255, 256 to 511, ...) at most 4 rows name the same one
- tile_offset: int32 [32768], P(('gx', 'gy')), may hold values from 0 to 8128, as said below
- closure: float32 [8, 16], replicated, may hold values from -1.5 to 1.5
- damping: float32 [8], replicated, may hold values from 0.5 to 1.5
Outputs:
- drag_field: bfloat16 [8, 64, 128, 128], P(None, 'gx', 'gy')
- particle_force: float32 [8, 1310720], P(None, ('gx', 'gy'))
Inputs may be any that keep to these rules, and one draw needn't show every extreme that they name: `migrant_index`: on each device the first migrant_count entries of its four rows name distinct particles of that device. `migrant_count`: some device's count reaches 512. `source_tile_size`: the sizes of one device sum to 12288. `tile_owner`: among the tiles of one device no owner is named more than 4 times, a bound that some block reaches. Every tile lies in one vertical column of its owner's block: tile_offset % 128 + 64 <= 128.
All inputs are finite; a program needn't handle non-finite values.
Results may differ from a plain program's by a relative error of at most 0.0053.
Values may be sent and summed in bfloat16 or wider, within the bound.
A program may use at most 64 MiB of HBM per device.

v0:
```python
import jax
import jax.numpy as jnp
from jax import lax
from jax.experimental import pallas as pl
from jax.experimental.pallas import tpu as pltpu
from jax.sharding import PartitionSpec as P

F32 = jnp.float32
BF16 = jnp.bfloat16
I32 = jnp.int32
MESH = pl.DeviceIdType.MESH

N_GX = 8
N_GY = 16
N = N_GX * N_GY
CH = 16
DR = 8
PART = 8192
MIG = 512
SLOTS = PART + 4 * MIG
TILES = 256
FX = 8
FY = 8
FZ = 128
W = 256
BLOCKS = SLOTS // W
RES = PART // W
PER = 4
CHUNKS = BLOCKS // PER
KC = PER * W
ND = 32
NB = N // ND
SB = 16
NSB = N // SB
HIGH = 32
SIDES = tuple((dx, dy) for dx in (-1, 0, 1) for dy in (-1, 0, 1) if dx or dy)


def dot_nn(a, b):
    return lax.dot_general(a, b, (((1,), (0,)), ((), ())), preferred_element_type=F32)


def dot_nt(a, b):
    return lax.dot_general(a, b, (((1,), (1,)), ((), ())), preferred_element_type=F32)


def iota(shape, dim):
    return lax.broadcasted_iota(I32, shape, dim)


def wait_bytes(ref, sem):
    pltpu.make_async_copy(ref, ref, sem).wait()


def body(
    part, midx, cnt, cell, size, owner, toff, clos, damp,
    drag_o, force_o,
    pt, smig, rmig, live, rel_a, rel_b, lall, m16s, den16s, abuf, acc,
    sendm, sendd, recvm, recvd, lg, low_s, high_s, gas, dtmp, tab, sendr, retm, rbuf,
    mig_ss, mig_rs, am_ss, am_rs, ad_ss, ad_rs, halo_ss, halo_rs, back_ss, back_rs,
):
    gx = lax.axis_index("gx")
    gy = lax.axis_index("gy")
    me = gx * N_GY + gy

    def ahead(rel):
        target = lax.rem(me + rel, N)
        return (lax.div(target, N_GY), lax.rem(target, N_GY))

    def beside(dx, dy):
        return (lax.rem(gx + dx + N_GX, N_GX), lax.rem(gy + dy + N_GY, N_GY))

    barrier = pltpu.get_barrier_semaphore()

    @pl.loop(1, N)
    def _(rel):
        pl.semaphore_signal(barrier, 1, device_id=ahead(rel), device_id_type=MESH)

    @pl.loop(0, RES)
    def _(g):
        lanes = pl.ds(pl.multiple_of(g * W, W), W)
        pt[pl.ds(pl.multiple_of(g * CH, CH), CH), :] = part[:, lanes].astype(BF16)

    hits = jnp.zeros((RES, W), F32)
    for j in range(4):
        entry = midx[j : j + 1, :]
        low = entry & (W - 1)
        high = entry >> 8
        valid = iota((1, MIG), 1) < cnt[0, j]
        low_hot = jnp.where(iota((W, MIG), 0) == low, 1.0, 0.0).astype(BF16)
        picked = dot_nn(pt[...], low_hot)
        state = jnp.zeros((CH, MIG), F32)
        high_b = jnp.broadcast_to(high, (CH, MIG))
        for g in range(RES):
            state = jnp.where(high_b == g, picked[g * CH : (g + 1) * CH], state)
        flag = jnp.where(valid, 1.0, 0.0)
        smig[j, 0:CH] = (state * flag).astype(BF16)
        smig[j, CH : 2 * CH] = jnp.broadcast_to(flag, (CH, MIG)).astype(BF16)
        high_hot = jnp.where(iota((RES, MIG), 0) == high, flag, 0.0).astype(BF16)
        hits = hits + dot_nt(high_hot, low_hot)
    live[0:RES] = 1.0 - hits

    pl.semaphore_wait(barrier, N - 1)
    mig = []
    for j, (dx, dy) in enumerate(((1, 0), (-1, 0), (0, 1), (0, -1))):
        copy = pltpu.make_async_remote_copy(
            smig.at[j], rmig.at[j], mig_ss.at[j], mig_rs.at[j],
            device_id=beside(dx, dy), device_id_type=MESH,
        )
        copy.start()
        mig.append(copy)

    sub = iota((TILES, TILES), 0)
    lane = iota((TILES, TILES), 1)
    size_row = size[...].astype(F32)
    own_row = owner[...].astype(F32)
    start_col = jnp.sum(jnp.where(lane < sub, size_row, 0.0), axis=1, keepdims=True)
    size_col = jnp.sum(jnp.where(lane == sub, size_row, 0.0), axis=1, keepdims=True)
    start_row = jnp.sum(jnp.where(sub < lane, size_col, 0.0), axis=0, keepdims=True)
    own_col = jnp.sum(jnp.where(lane == sub, own_row, 0.0), axis=1, keepdims=True)
    earlier = jnp.where(own_col == own_row, jnp.where(sub < lane, 1.0, 0.0), 0.0)
    rank_row = jnp.sum(earlier, axis=0, keepdims=True)
    rel_row = own_row - me.astype(F32)
    rel_row = jnp.where(rel_row < 0.0, rel_row + N, rel_row)
    base_row = 64.0 * rank_row - start_row
    sub8 = iota((8, TILES), 0)
    values = jnp.where(sub8 == 0, rel_row, jnp.where(sub8 == 1, base_row, 0.0))
    before = jnp.where(iota((8, TILES), 1) == 0, 0.0, pltpu.roll(values, 1, 1))
    steps = (values - before).astype(BF16)

    offs = toff[...]
    xx = offs >> 10
    off_low = ((xx & 1) * FZ + (offs & (FZ - 1))).astype(F32)
    off_high = ((xx >> 1) * FY + ((offs >> 7) & (FY - 1))).astype(F32)
    sub128 = iota((N, TILES), 0)
    rank_of = (sub128 & 3).astype(F32)
    what = jnp.where(sub128 < 4, off_low, jnp.where(sub128 < 8, off_high, 0.0))
    what = jnp.where(rank_row == rank_of, what, 0.0).astype(BF16)
    rel_hot = jnp.where(sub128.astype(F32) == rel_row, 1.0, 0.0).astype(BF16)
    meta = dot_nt(rel_hot, what)
    for d in range(N):
        sendd[d, :, W : W + 128] = meta[d : d + 1, :]

    clos_f = clos[...]
    clos_hi = clos_f.astype(BF16)
    clos_lo = (clos_f - clos_hi.astype(F32)).astype(BF16)
    clos2 = jnp.concatenate([clos_hi.astype(F32), clos_lo.astype(F32)], axis=0).astype(BF16)

    sub16 = iota((16, W), 0)

    def prepare(g, dep):
        row = jnp.concatenate([cell[pl.ds(2 * g, 1), :], cell[pl.ds(2 * g + 1, 1), :]], axis=1)
        row = row.astype(F32)
        inside = jnp.where(start_col <= row, 1.0, 0.0).astype(BF16)
        found = dot_nn(steps, inside)
        rel = found[0:1]
        place = row + found[1:2]
        hot = jnp.where(iota((W, W), 0).astype(F32) == place, 1.0, 0.0).astype(BF16)
        lall[lax.div(g, PER), :, pl.ds(pl.multiple_of(lax.rem(g, PER) * W, W), W)] = hot
        rel_a[g] = (rel - jnp.where(sub16 >= 8, 1.0, 0.0)).astype(BF16)
        rel_b[g] = (rel - sub16.astype(F32)).astype(BF16)
        mixed = dot_nn(clos2, dep)
        mixed = mixed[0:8] + mixed[8:16]
        m16s[g] = jnp.concatenate([mixed, mixed], axis=0).astype(BF16)
        den16s[g] = jnp.broadcast_to(dep[0:1].astype(F32), (16, W)).astype(BF16)

    @pl.loop(0, RES)
    def _(g):
        lanes = pl.ds(pl.multiple_of(g * W, W), W)
        prepare(g, (part[:, lanes] * live[pl.ds(g, 1), :]).astype(BF16))

    for copy in mig:
        copy.wait_recv()
    for j in range(4):
        for h in range(2):
            g = RES + 2 * j + h
            live[g : g + 1] = rmig[j, CH : 2 * CH, h * W : (h + 1) * W].astype(F32)[0:1]
            prepare(g, rmig[j, 0:CH, h * W : (h + 1) * W])

    zero16 = jnp.zeros((16, W), BF16)
    for block in range(NB):
        @pl.loop(0, CHUNKS)
        def _(c):
            for i in range(PER):
                g = c * PER + i
                at = slice(i * W, (i + 1) * W)
                near, m16 = rel_a[g], m16s[g]
                for k in range(ND // 2):
                    abuf[k * 16 : (k + 1) * 16, at] = jnp.where(
                        near == float(block * ND + 2 * k), m16, zero16
                    )
                near, den = rel_b[g], den16s[g]
                for k in range(ND // 16):
                    abuf[ND * 8 + k * 16 : ND * 8 + (k + 1) * 16, at] = jnp.where(
                        near == float(block * ND + 16 * k), den, zero16
                    )
            part_sum = dot_nt(abuf[0 : ND * 9], lall[c])

            @pl.when(c == 0)
            def _():
                acc[0 : ND * 9] = part_sum

            @pl.when(c > 0)
            def _():
                acc[0 : ND * 9] += part_sum

        sendm[block * ND : (block + 1) * ND] = (
            acc[0 : ND * 8].reshape(ND, 8, W).astype(BF16)
        )
        den = acc[ND * 8 : ND * 9]
        for d in range(ND):
            sendd[block * ND + d, :, 0:W] = den[d : d + 1]
        if block == 0:
            recvm[0] = sendm[0]
            recvd[0] = sendd[0]

        @pl.loop(1 if block == 0 else block * ND, (block + 1) * ND)
        def _(rel):
            sb = lax.div(rel, SB)
            target = ahead(rel)
            pltpu.make_async_remote_copy(
                sendm.at[rel], recvm.at[rel], am_ss.at[sb], am_rs.at[sb],
                device_id=target, device_id_type=MESH,
            ).start()
            pltpu.make_async_remote_copy(
                sendd.at[rel], recvd.at[rel], ad_ss.at[sb], ad_rs.at[sb],
                device_id=target, device_id_type=MESH,
            ).start()

    def span(b):
        return pl.ds(1, SB - 1) if b == 0 else pl.ds(b * SB, SB)

    lane_row = iota((1, W), 1)
    inner = (lane_row & 63).astype(F32)
    which = lane_row >> 6
    for b in range(NSB):
        wait_bytes(recvm.at[span(b)], am_rs.at[b])
        wait_bytes(recvd.at[span(b)], ad_rs.at[b])

        @pl.loop(0, SB // PER)
        def _(q):
            for i in range(PER):
                s = b * SB + q * PER + i
                at = slice(i * W, (i + 1) * W)
                small = recvd[s]
                low = jnp.zeros((1, W), F32)
                high = jnp.zeros((1, W), F32)
                for j in range(4):
                    low = jnp.where(which == j, small[:, W + j : W + j + 1], low)
                    high = jnp.where(which == j, small[:, W + 4 + j : W + 5 + j], high)
                low = low + inner
                high_s[s] = high
                hot = jnp.where(iota((W, W), 0).astype(F32) == low, 1.0, 0.0).astype(BF16)
                lg[b * (SB // PER) + q, :, at] = hot
                mixed = recvm[s].astype(F32)
                m16 = jnp.concatenate([mixed, mixed], axis=0).astype(BF16)
                near = (high - jnp.where(sub16 >= 8, 1.0, 0.0)).astype(BF16)
                for k in range(HIGH // 2):
                    abuf[k * 16 : (k + 1) * 16, at] = jnp.where(near == float(2 * k), m16, zero16)
                den = jnp.broadcast_to(small[:, 0:W], (16, W)).astype(BF16)
                near = (high - sub16.astype(F32)).astype(BF16)
                for k in range(HIGH // 16):
                    abuf[HIGH * 8 + k * 16 : HIGH * 8 + (k + 1) * 16, at] = jnp.where(
                        near == float(16 * k), den, zero16
                    )
            part_sum = dot_nt(abuf[0 : HIGH * 9], lg[b * (SB // PER) + q])
            if b == 0:
                @pl.when(q == 0)
                def _():
                    acc[0 : HIGH * 9] = part_sum

                @pl.when(q > 0)
                def _():
                    acc[0 : HIGH * 9] += part_sum
            else:
                acc[0 : HIGH * 9] += part_sum

    for h in range(HIGH):
        for odd in range(2):
            x, y = 2 * (h // FY) + odd + 1, h % FY + 1
            at = slice(odd * FZ, (odd + 1) * FZ)
            gas[x, y, 0:8] = acc[h * 8 : (h + 1) * 8, at]
            gas[x, y, 8:16] = jnp.broadcast_to(acc[HIGH * 8 + h : HIGH * 8 + h + 1, at], (8, FZ))

    def edge(step, far):
        if step == 0:
            return pl.ds(1, 8)
        if far:
            return pl.ds(0 if step > 0 else 9, 1)
        return pl.ds(8 if step > 0 else 1, 1)

    halo = []
    for i, (dx, dy) in enumerate(SIDES):
        copy = pltpu.make_async_remote_copy(
            gas.at[edge(dx, False), edge(dy, False)], gas.at[edge(dx, True), edge(dy, True)],
            halo_ss.at[i], halo_rs.at[i], device_id=beside(dx, dy), device_id_type=MESH,
        )
        copy.start()
        halo.append(copy)
    for copy in halo:
        copy.wait_recv()

    @pl.loop(0, FX // 2)
    def _(x2):
        for odd in range(2):
            x = 2 * x2 + odd
            over_x = [gas[x, y] + 2.0 * gas[x + 1, y] + gas[x + 2, y] for y in range(FY + 2)]
            got = []
            for y in range(FY):
                smooth = (over_x[y] + 2.0 * over_x[y + 1] + over_x[y + 2]) * (1.0 / 16.0)
                dens = smooth[8:16]
                drag = smooth[0:8] / (1.0 + dens * dens)
                dtmp[x, y * 8 : (y + 1) * 8] = drag
                got.append(drag)
            for y in range(0, FY, 2):
                tab[pl.ds(pl.multiple_of(x2 * 64 + y * 8, 16), 16), odd * FZ : (odd + 1) * FZ] = (
                    jnp.concatenate([got[y], got[y + 1]], axis=0).astype(BF16)
                )

    for b in range(NSB):
        @pl.loop(0, SB // PER)
        def _(q):
            for i in range(PER):
                s = b * SB + q * PER + i
                at = slice(i * W, (i + 1) * W)
                full = dot_nn(tab[...], lg[b * (SB // PER) + q, :, at])
                high = jnp.broadcast_to(high_s[s], (8, W))
                got = jnp.zeros((8, W), F32)
                for h in range(HIGH):
                    got = jnp.where(high == float(h), full[h * 8 : (h + 1) * 8], got)
                sendr[s] = got.astype(BF16)

        if b == 0:
            retm[0] = sendr[0]

        @pl.loop(1 if b == 0 else b * SB, (b + 1) * SB)
        def _(rel):
            pltpu.make_async_remote_copy(
                sendr.at[rel], retm.at[rel], back_ss.at[b], back_rs.at[b],
                device_id=ahead(N - rel), device_id_type=MESH,
            ).start()

    for r in range(DR):
        for x in range(FX):
            drag_o[r, x] = dtmp[x, pl.ds(r, FY, stride=8), :].astype(BF16)

    for b in range(NSB):
        wait_bytes(retm.at[span(b)], back_rs.at[b])
        back = retm[b * SB : (b + 1) * SB].astype(F32).reshape(SB * 8, W)
        rbuf[b * SB * 8 : (b + 1) * SB * 8] = back.astype(BF16)

    rows8 = iota((8, W), 0)
    slip = jnp.zeros((8, W), F32)
    for r in range(DR):
        slip = jnp.where(rows8 == r, damp[r], slip)

    def finish(g, c, i, state):
        hot = lall[c, :, i * W : (i + 1) * W]
        rel = jnp.broadcast_to(rel_a[g].astype(F32)[0:1], (8, W))
        got = jnp.zeros((8, W), F32)
        for b in range(NSB):
            full = dot_nn(rbuf[b * SB * 8 : (b + 1) * SB * 8], hot)
            for d in range(SB):
                got = jnp.where(rel == float(b * SB + d), full[d * 8 : (d + 1) * 8], got)
        force_o[:, pl.ds(pl.multiple_of(g * W, W), W)] = live[pl.ds(g, 1), :] * (
            got - slip * state
        )

    @pl.loop(0, RES // PER)
    def _(c):
        for i in range(PER):
            g = c * PER + i
            finish(g, c, i, part[0:8, pl.ds(pl.multiple_of(g * W, W), W)])

    for j in range(4):
        for h in range(2):
            g = RES + 2 * j + h
            finish(g, g // PER, g % PER, rmig[j, 0:CH, h * W : (h + 1) * W].astype(F32)[0:8])

    for copy in mig + halo:
        copy.wait_send()
    for b in range(NSB):
        wait_bytes(sendm.at[span(b)], am_ss.at[b])
        wait_bytes(sendd.at[span(b)], ad_ss.at[b])
        wait_bytes(sendr.at[span(b)], back_ss.at[b])


def per_device(
    particles, migrant_index, migrant_count, migrated_slot_cell, source_tile_size,
    tile_owner, tile_offset, closure, damping,
):
    vmem = pl.BlockSpec(memory_space=pltpu.VMEM)
    smem = pl.BlockSpec(memory_space=pltpu.SMEM)
    dma = pltpu.SemaphoreType.DMA
    scratch = [
        pltpu.VMEM((RES * CH, W), BF16),
        pltpu.VMEM((4, 2 * CH, MIG), BF16),
        pltpu.VMEM((4, 2 * CH, MIG), BF16),
        pltpu.VMEM((BLOCKS, W), F32),
        pltpu.VMEM((BLOCKS, 16, W), BF16),
        pltpu.VMEM((BLOCKS, 16, W), BF16),
        pltpu.VMEM((CHUNKS, W, KC), BF16),
        pltpu.VMEM((BLOCKS, 16, W), BF16),
        pltpu.VMEM((BLOCKS, 16, W), BF16),
        pltpu.VMEM((max(ND, HIGH) * 9, KC), BF16),
        pltpu.VMEM((max(ND, HIGH) * 9, W), F32),
        pltpu.VMEM((N, 8, W), BF16),
        pltpu.VMEM((N, 1, W + 128), F32),
        pltpu.VMEM((N, 8, W), BF16),
        pltpu.VMEM((N, 1, W + 128), F32),
        pltpu.VMEM((N // PER, W, KC), BF16),
        pltpu.VMEM((8, 128), F32),
        pltpu.VMEM((N, 1, W), F32),
        pltpu.VMEM((FX + 2, FY + 2, 16, FZ), F32),
        pltpu.VMEM((FX, FY * 8, FZ), F32),
        pltpu.VMEM((HIGH * 8, W), BF16),
        pltpu.VMEM((N, 8, W), BF16),
        pltpu.VMEM((N, 8, W), BF16),
        pltpu.VMEM((N * 8, W), BF16),
        dma((4,)), dma((4,)), dma((NSB,)), dma((NSB,)), dma((NSB,)), dma((NSB,)),
        dma((8,)), dma((8,)), dma((NSB,)), dma((NSB,)),
    ]
    return pl.pallas_call(
        body,
        out_shape=(
            jax.ShapeDtypeStruct((DR, FX, FY, FZ), BF16),
            jax.ShapeDtypeStruct((DR, SLOTS), F32),
        ),
        in_specs=[vmem, vmem, smem, vmem, vmem, vmem, vmem, vmem, smem],
        out_specs=(vmem, vmem),
        scratch_shapes=scratch,
        compiler_params=pltpu.CompilerParams(
            collective_id=0, has_side_effects=True, vmem_limit_bytes=60 * 1024 * 1024
        ),
    )(
        particles,
        migrant_index,
        migrant_count,
        migrated_slot_cell.reshape(2 * BLOCKS, 128),
        source_tile_size,
        tile_owner.reshape(1, TILES),
        tile_offset.reshape(1, TILES),
        closure,
        damping,
    )


def solution(mesh):
    in_specs = (
        P(None, ("gx", "gy")),
        P(("gx", "gy"), None),
        P(("gx", "gy"), None),
        P(("gx", "gy")),
        P(("gx", "gy"), None),
        P(("gx", "gy"), None),
        P(("gx", "gy")),
        P(),
        P(),
    )
    out_specs = (P(None, "gx", "gy", None), P(None, ("gx", "gy")))
    return jax.shard_map(
        per_device, mesh=mesh, in_specs=in_specs, out_specs=out_specs, check_vma=False
    )
```

profile of v0, /device:TPU:1, one launch (start us, length us, event | category | flops | bytes accessed | tf_op | source)
XLA Modules:
  0.0 86.3 jit_solution(7570006868099717744)
XLA Ops:
  0.6 82.3 %shard_map.104 = (bf16[8,8,8,128]{3,2,1,0:T(8,128)(2,1)}, f32[8,10240]{1,0:T(8,128)}) custom-call(f32[16,8192]{1,0:T(8,128)} %part.1, s32[4,512]{1,0:T(4,128)} %midx.1, s32[1,4]{1,0:T(1,128)} %cnt.1, s32[80,128]{1,0:T(8,128)} %bitcast.3, s32[1,256]{1,0:T(1,128)} %size.1, s32[1,256]{1,0:T(1,128)} %bitcast.4, s32[1,256]{1,0:T(1,128)} %bitcast.5, ...), custom_call_target="tpu_custom_call" | custom-call | tf_op jit(solution)/shard_map/pallas_call | solution.py:423
  83.0 1.6 %copy.13 = bf16[8,8,8,128]{3,2,1,0:T(8,128)(2,1)} copy(bf16[8,8,8,128]{3,2,1,0:T(8,128)(2,1)} %get-tuple-element.4) | data formatting | bytes 262144
  84.5 1.7 %copy.14 = f32[8,10240]{1,0:T(8,128)} copy(f32[8,10240]{1,0:T(8,128)} %get-tuple-element.5) | data formatting | bytes 655360
where the time goes:
time: 86.4 us; the launch traced here: 86.3 us
  Pallas kernels  82.3 us (95%)
  local copies, waits for them, and re-layouts  3.29 us (4%)
    pallas_call x1, Pallas kernels, per_device(): pl.pallas_call(body, out_shape=(jax.ShapeDtypeStruct((DR, FX, FY, FZ), BF...  82.3 us
    unnamed x2, local copies, waits for them, and re-layouts  3.29 us

commit v1 on v0

--- a/solution.py
+++ b/solution.py
@@ -25,6 +25,8 @@
 W = 256
 BLOCKS = SLOTS // W
 RES = PART // W
+RCH = 8
+LATE = 0
 PER = 4
 CHUNKS = BLOCKS // PER
 KC = PER * W
@@ -32,7 +34,10 @@
 NB = N // ND
 SB = 16
 NSB = N // SB
-HIGH = 32
+UN = 4
+HOP = 37
+BACK = 45
+EXT = 128
 SIDES = tuple((dx, dy) for dx in (-1, 0, 1) for dy in (-1, 0, 1) if dx or dy)
 
 
@@ -46,6 +51,10 @@
 
 def iota(shape, dim):
     return lax.broadcasted_iota(I32, shape, dim)
+
+
+def tiles2(tiles, r):
+    return tiles.reshape(4 * N * 8, FZ)[pl.ds(r, 4 * N, stride=8), :].astype(BF16)
 
 
 def wait_bytes(ref, sem):
@@ -56,19 +65,19 @@
     part, midx, cnt, cell, size, owner, toff, clos, damp,
     drag_o, force_o,
     pt, smig, rmig, live, rel_a, rel_b, lall, m16s, den16s, abuf, acc,
-    sendm, sendd, recvm, recvd, lg, low_s, high_s, gas, dtmp, tab, sendr, retm, rbuf,
-    mig_ss, mig_rs, am_ss, am_rs, ad_ss, ad_rs, halo_ss, halo_rs, back_ss, back_rs,
+    sendm, ext, recvm, meta_v, meta_s, tiles, tden, flat, picked, gas, dtmp, sendr, retm, rbuf,
+    mig_ss, mig_rs, am_ss, am_rs, halo_ss, halo_rs, back_ss, back_rs, meta_sem,
 ):
     gx = lax.axis_index("gx")
     gy = lax.axis_index("gy")
     me = gx * N_GY + gy
 
     def ahead(rel):
-        target = lax.rem(me + rel, N)
-        return (lax.div(target, N_GY), lax.rem(target, N_GY))
+        target = (me + rel * HOP) & (N - 1)
+        return (target >> 4, target & (N_GY - 1))
 
     def beside(dx, dy):
-        return (lax.rem(gx + dx + N_GX, N_GX), lax.rem(gy + dy + N_GY, N_GY))
+        return ((gx + dx) & (N_GX - 1), (gy + dy) & (N_GY - 1))
 
     barrier = pltpu.get_barrier_semaphore()
 
@@ -88,11 +97,11 @@
         high = entry >> 8
         valid = iota((1, MIG), 1) < cnt[0, j]
         low_hot = jnp.where(iota((W, MIG), 0) == low, 1.0, 0.0).astype(BF16)
-        picked = dot_nn(pt[...], low_hot)
+        found = dot_nn(pt[...], low_hot)
         state = jnp.zeros((CH, MIG), F32)
         high_b = jnp.broadcast_to(high, (CH, MIG))
         for g in range(RES):
-            state = jnp.where(high_b == g, picked[g * CH : (g + 1) * CH], state)
+            state = jnp.where(high_b == g, found[g * CH : (g + 1) * CH], state)
         flag = jnp.where(valid, 1.0, 0.0)
         smig[j, 0:CH] = (state * flag).astype(BF16)
         smig[j, CH : 2 * CH] = jnp.broadcast_to(flag, (CH, MIG)).astype(BF16)
@@ -120,8 +129,7 @@
     own_col = jnp.sum(jnp.where(lane == sub, own_row, 0.0), axis=1, keepdims=True)
     earlier = jnp.where(own_col == own_row, jnp.where(sub < lane, 1.0, 0.0), 0.0)
     rank_row = jnp.sum(earlier, axis=0, keepdims=True)
-    rel_row = own_row - me.astype(F32)
-    rel_row = jnp.where(rel_row < 0.0, rel_row + N, rel_row)
+    rel_row = (((owner[...] - me) * BACK) & (N - 1)).astype(F32)
     base_row = 64.0 * rank_row - start_row
     sub8 = iota((8, TILES), 0)
     values = jnp.where(sub8 == 0, rel_row, jnp.where(sub8 == 1, base_row, 0.0))
@@ -129,17 +137,16 @@
     steps = (values - before).astype(BF16)
 
     offs = toff[...]
-    xx = offs >> 10
-    off_low = ((xx & 1) * FZ + (offs & (FZ - 1))).astype(F32)
-    off_high = ((xx >> 1) * FY + ((offs >> 7) & (FY - 1))).astype(F32)
+    off_low = (offs & (FZ - 1)).astype(F32)
+    off_high = (offs >> 7).astype(F32)
     sub128 = iota((N, TILES), 0)
     rank_of = (sub128 & 3).astype(F32)
     what = jnp.where(sub128 < 4, off_low, jnp.where(sub128 < 8, off_high, 0.0))
     what = jnp.where(rank_row == rank_of, what, 0.0).astype(BF16)
     rel_hot = jnp.where(sub128.astype(F32) == rel_row, 1.0, 0.0).astype(BF16)
     meta = dot_nt(rel_hot, what)
-    for d in range(N):
-        sendd[d, :, W : W + 128] = meta[d : d + 1, :]
+    for d in range(0, N, 8):
+        ext[pl.ds(d * 8 + 4, 8, stride=8), :] = meta[d : d + 8]
 
     clos_f = clos[...]
     clos_hi = clos_f.astype(BF16)
@@ -169,6 +176,33 @@
         lanes = pl.ds(pl.multiple_of(g * W, W), W)
         prepare(g, (part[:, lanes] * live[pl.ds(g, 1), :]).astype(BF16))
 
+    zero16 = jnp.zeros((16, W), BF16)
+
+    def spread(c, first, count, row0):
+        for i in range(PER):
+            g = c * PER + i
+            at = slice(i * W, (i + 1) * W)
+            near, m16 = rel_a[g], m16s[g]
+            for k in range(count // 2):
+                abuf[row0 + k * 16 : row0 + (k + 1) * 16, at] = jnp.where(
+                    near == float(first + 2 * k), m16, zero16
+                )
+            near, den = rel_b[g], den16s[g]
+            for k in range(count // 16):
+                abuf[row0 + count * 8 + k * 16 : row0 + count * 8 + (k + 1) * 16, at] = jnp.where(
+                    near == float(first + 16 * k), den, zero16
+                )
+
+    def resident(c):
+        spread(c, 0, N, 0)
+        return dot_nt(abuf[...], lall[c])
+
+    acc[...] = jnp.zeros(acc.shape, F32)
+
+    @pl.loop(0, RCH - LATE)
+    def _(c):
+        acc[...] += resident(c)
+
     for copy in mig:
         copy.wait_recv()
     for j in range(4):
@@ -177,110 +211,99 @@
             live[g : g + 1] = rmig[j, CH : 2 * CH, h * W : (h + 1) * W].astype(F32)[0:1]
             prepare(g, rmig[j, 0:CH, h * W : (h + 1) * W])
 
-    zero16 = jnp.zeros((16, W), BF16)
+    def send_out(rel):
+        sb = lax.div(rel, SB)
+        pltpu.make_async_remote_copy(
+            sendm.at[rel], recvm.at[rel], am_ss.at[sb], am_rs.at[sb],
+            device_id=ahead(rel), device_id_type=MESH,
+        ).start()
+
     for block in range(NB):
-        @pl.loop(0, CHUNKS)
-        def _(c):
-            for i in range(PER):
-                g = c * PER + i
-                at = slice(i * W, (i + 1) * W)
-                near, m16 = rel_a[g], m16s[g]
-                for k in range(ND // 2):
-                    abuf[k * 16 : (k + 1) * 16, at] = jnp.where(
-                        near == float(block * ND + 2 * k), m16, zero16
-                    )
-                near, den = rel_b[g], den16s[g]
-                for k in range(ND // 16):
-                    abuf[ND * 8 + k * 16 : ND * 8 + (k + 1) * 16, at] = jnp.where(
-                        near == float(block * ND + 16 * k), den, zero16
-                    )
-            part_sum = dot_nt(abuf[0 : ND * 9], lall[c])
-
-            @pl.when(c == 0)
-            def _():
-                acc[0 : ND * 9] = part_sum
-
-            @pl.when(c > 0)
-            def _():
-                acc[0 : ND * 9] += part_sum
-
-        sendm[block * ND : (block + 1) * ND] = (
-            acc[0 : ND * 8].reshape(ND, 8, W).astype(BF16)
-        )
-        den = acc[ND * 8 : ND * 9]
-        for d in range(ND):
-            sendd[block * ND + d, :, 0:W] = den[d : d + 1]
+        rows = slice(block * ND * 8, (block + 1) * ND * 8)
+        drows = slice(N * 8 + block * ND, N * 8 + (block + 1) * ND)
+        mixed = acc[rows]
+        den = acc[drows]
+        for c in range(RCH, CHUNKS):
+            base = (c - RCH) * ND * 9
+            spread(c, block * ND, ND, base)
+            more = dot_nt(abuf[base : base + ND * 9], lall[c])
+            mixed = mixed + more[0 : ND * 8]
+            den = den + more[ND * 8 : ND * 9]
+        sendm[block * ND : (block + 1) * ND, :, 0:W] = mixed.reshape(ND, 8, W).astype(BF16)
+        den_hi = den.astype(BF16).astype(F32)
+        den_lo = den - den_hi
+        for d in range(0, ND, 8):
+            row = (block * ND + d) * 8
+            for half in range(2):
+                at = slice(half * 128, (half + 1) * 128)
+                ext[pl.ds(row + half, 8, stride=8), :] = den_hi[d : d + 8, at]
+                ext[pl.ds(row + 2 + half, 8, stride=8), :] = den_lo[d : d + 8, at]
+        sendm[block * ND : (block + 1) * ND, :, W : W + EXT] = (
+            ext[rows].reshape(ND, 8, EXT).astype(BF16)
+        )
         if block == 0:
             recvm[0] = sendm[0]
-            recvd[0] = sendd[0]
 
         @pl.loop(1 if block == 0 else block * ND, (block + 1) * ND)
         def _(rel):
-            sb = lax.div(rel, SB)
-            target = ahead(rel)
-            pltpu.make_async_remote_copy(
-                sendm.at[rel], recvm.at[rel], am_ss.at[sb], am_rs.at[sb],
-                device_id=target, device_id_type=MESH,
-            ).start()
-            pltpu.make_async_remote_copy(
-                sendd.at[rel], recvd.at[rel], ad_ss.at[sb], ad_rs.at[sb],
-                device_id=target, device_id_type=MESH,
-            ).start()
+            send_out(rel)
 
     def span(b):
         return pl.ds(1, SB - 1) if b == 0 else pl.ds(b * SB, SB)
 
-    lane_row = iota((1, W), 1)
-    inner = (lane_row & 63).astype(F32)
-    which = lane_row >> 6
+    lane_row = iota((1, FZ), 1)
+    first_half = lane_row < 64
     for b in range(NSB):
         wait_bytes(recvm.at[span(b)], am_rs.at[b])
-        wait_bytes(recvd.at[span(b)], ad_rs.at[b])
-
-        @pl.loop(0, SB // PER)
-        def _(q):
-            for i in range(PER):
-                s = b * SB + q * PER + i
-                at = slice(i * W, (i + 1) * W)
-                small = recvd[s]
-                low = jnp.zeros((1, W), F32)
-                high = jnp.zeros((1, W), F32)
-                for j in range(4):
-                    low = jnp.where(which == j, small[:, W + j : W + j + 1], low)
-                    high = jnp.where(which == j, small[:, W + 4 + j : W + 5 + j], high)
-                low = low + inner
-                high_s[s] = high
-                hot = jnp.where(iota((W, W), 0).astype(F32) == low, 1.0, 0.0).astype(BF16)
-                lg[b * (SB // PER) + q, :, at] = hot
-                mixed = recvm[s].astype(F32)
-                m16 = jnp.concatenate([mixed, mixed], axis=0).astype(BF16)
-                near = (high - jnp.where(sub16 >= 8, 1.0, 0.0)).astype(BF16)
-                for k in range(HIGH // 2):
-                    abuf[k * 16 : (k + 1) * 16, at] = jnp.where(near == float(2 * k), m16, zero16)
-                den = jnp.broadcast_to(small[:, 0:W], (16, W)).astype(BF16)
-                near = (high - sub16.astype(F32)).astype(BF16)
-                for k in range(HIGH // 16):
-                    abuf[HIGH * 8 + k * 16 : HIGH * 8 + (k + 1) * 16, at] = jnp.where(
-                        near == float(16 * k), den, zero16
-                    )
-            part_sum = dot_nt(abuf[0 : HIGH * 9], lg[b * (SB // PER) + q])
-            if b == 0:
-                @pl.when(q == 0)
-                def _():
-                    acc[0 : HIGH * 9] = part_sum
-
-                @pl.when(q > 0)
-                def _():
-                    acc[0 : HIGH * 9] += part_sum
-            else:
-                acc[0 : HIGH * 9] += part_sum
-
-    for h in range(HIGH):
-        for odd in range(2):
-            x, y = 2 * (h // FY) + odd + 1, h % FY + 1
-            at = slice(odd * FZ, (odd + 1) * FZ)
-            gas[x, y, 0:8] = acc[h * 8 : (h + 1) * 8, at]
-            gas[x, y, 8:16] = jnp.broadcast_to(acc[HIGH * 8 + h : HIGH * 8 + h + 1, at], (8, FZ))
+        ext[b * SB * 8 : (b + 1) * SB * 8] = (
+            recvm[b * SB : (b + 1) * SB, :, W : W + EXT].astype(F32).reshape(SB * 8, EXT)
+        )
+        meta_v[b * SB : (b + 1) * SB] = ext[pl.ds(b * SB * 8 + 4, SB, stride=8), :].astype(I32)
+        pltpu.make_async_copy(
+            meta_v.at[pl.ds(b * SB, SB)], meta_s.at[pl.ds(b * SB, SB)], meta_sem.at[b]
+        ).start()
+
+    for b in range(NSB):
+        wait_bytes(meta_s.at[pl.ds(b * SB, SB)], meta_sem.at[b])
+
+    @pl.loop(0, N // UN)
+    def _(q):
+        for i in range(UN):
+            s = q * UN + i
+            whole = recvm[s, :, 0:W].astype(F32)
+            for j in range(4):
+                half = j // 2
+                keep = first_half if j % 2 == 0 else ~first_half
+                shift = (meta_s[s, j] + (0 if j % 2 == 0 else 64)) & (FZ - 1)
+                at = slice(half * FZ, (half + 1) * FZ)
+                tiles[j * N + s] = pltpu.roll(jnp.where(keep, whole[:, at], 0.0), shift, 1)
+                den = ext[pl.ds(s * 8 + half, 1), :] + ext[pl.ds(s * 8 + 2 + half, 1), :]
+                den = jnp.broadcast_to(jnp.where(keep, den, 0.0), (8, FZ))
+                tden[pl.ds(j * N + s, 1), :] = pltpu.roll(den, shift, 1)[0:1]
+
+    square = iota((N, N), 0) == iota((N, N), 1)
+    meta_f = meta_v[...].astype(F32)
+    cols = []
+    for j in range(4):
+        cols.append(
+            jnp.sum(jnp.where(square, meta_f[:, 4 + j : 5 + j], 0.0), axis=0, keepdims=True)
+        )
+    col_row = jnp.concatenate(cols, axis=1)
+    col_hot = jnp.where(iota((FX * FY, 4 * N), 0).astype(F32) == col_row, 1.0, 0.0)
+    for r in range(0, DR, 2):
+        pair = [tiles2(tiles, r), tiles2(tiles, r + 1)]
+        sums = dot_nn(col_hot.astype(BF16), jnp.concatenate(pair, axis=1))
+        flat[r * 64 : (r + 1) * 64] = sums[:, 0:FZ]
+        flat[(r + 1) * 64 : (r + 2) * 64] = sums[:, FZ : 2 * FZ]
+    den = lax.dot_general(
+        col_hot, tden[...], (((1,), (0,)), ((), ())),
+        precision=lax.Precision.HIGHEST, preferred_element_type=F32,
+    )
+    for x in range(FX):
+        for y in range(FY):
+            c = x * FY + y
+            gas[x + 1, y + 1, 0:8] = flat[pl.ds(c, 8, stride=64), :]
+            gas[x + 1, y + 1, 8:16] = jnp.broadcast_to(den[c : c + 1], (8, FZ))
 
     def edge(step, far):
         if step == 0:
@@ -305,30 +328,41 @@
         for odd in range(2):
             x = 2 * x2 + odd
             over_x = [gas[x, y] + 2.0 * gas[x + 1, y] + gas[x + 2, y] for y in range(FY + 2)]
-            got = []
             for y in range(FY):
                 smooth = (over_x[y] + 2.0 * over_x[y + 1] + over_x[y + 2]) * (1.0 / 16.0)
                 dens = smooth[8:16]
                 drag = smooth[0:8] / (1.0 + dens * dens)
                 dtmp[x, y * 8 : (y + 1) * 8] = drag
-                got.append(drag)
-            for y in range(0, FY, 2):
-                tab[pl.ds(pl.multiple_of(x2 * 64 + y * 8, 16), 16), odd * FZ : (odd + 1) * FZ] = (
-                    jnp.concatenate([got[y], got[y + 1]], axis=0).astype(BF16)
-                )
+
+    tile_hot = jnp.concatenate(
+        [
+            jnp.where(iota((N, FX * FY), 1).astype(F32) == meta_f[:, 4 + j : 5 + j], 1.0, 0.0)
+            for j in range(4)
+        ],
+        axis=0,
+    ).astype(BF16)
+    drag_rows = dtmp.reshape(FX * FY * 8, FZ)
+    for r in range(0, DR, 2):
+        pair = [drag_rows[pl.ds(r + k, FX * FY, stride=8), :].astype(BF16) for k in range(2)]
+        got = dot_nn(tile_hot, jnp.concatenate(pair, axis=1))
+        picked[r * 4 * N : (r + 1) * 4 * N] = got[:, 0:FZ]
+        picked[(r + 1) * 4 * N : (r + 2) * 4 * N] = got[:, FZ : 2 * FZ]
 
     for b in range(NSB):
-        @pl.loop(0, SB // PER)
+        @pl.loop(0, SB // UN)
         def _(q):
-            for i in range(PER):
-                s = b * SB + q * PER + i
-                at = slice(i * W, (i + 1) * W)
-                full = dot_nn(tab[...], lg[b * (SB // PER) + q, :, at])
-                high = jnp.broadcast_to(high_s[s], (8, W))
-                got = jnp.zeros((8, W), F32)
-                for h in range(HIGH):
-                    got = jnp.where(high == float(h), full[h * 8 : (h + 1) * 8], got)
-                sendr[s] = got.astype(BF16)
+            for i in range(UN):
+                s = b * SB + q * UN + i
+                halves = []
+                for half in range(2):
+                    pair = []
+                    for j in (2 * half, 2 * half + 1):
+                        shift = ((0 if j % 2 == 0 else 64) - meta_s[s, j]) & (FZ - 1)
+                        pair.append(
+                            pltpu.roll(picked[pl.ds(j * N + s, 8, stride=4 * N), :], shift, 1)
+                        )
+                    halves.append(jnp.where(first_half, pair[0], pair[1]))
+                sendr[s] = jnp.concatenate(halves, axis=1).astype(BF16)
 
         if b == 0:
             retm[0] = sendr[0]
@@ -381,7 +415,6 @@
         copy.wait_send()
     for b in range(NSB):
         wait_bytes(sendm.at[span(b)], am_ss.at[b])
-        wait_bytes(sendd.at[span(b)], ad_ss.at[b])
         wait_bytes(sendr.at[span(b)], back_ss.at[b])
 
 
@@ -402,23 +435,24 @@
         pltpu.VMEM((CHUNKS, W, KC), BF16),
         pltpu.VMEM((BLOCKS, 16, W), BF16),
         pltpu.VMEM((BLOCKS, 16, W), BF16),
-        pltpu.VMEM((max(ND, HIGH) * 9, KC), BF16),
-        pltpu.VMEM((max(ND, HIGH) * 9, W), F32),
-        pltpu.VMEM((N, 8, W), BF16),
-        pltpu.VMEM((N, 1, W + 128), F32),
-        pltpu.VMEM((N, 8, W), BF16),
-        pltpu.VMEM((N, 1, W + 128), F32),
-        pltpu.VMEM((N // PER, W, KC), BF16),
-        pltpu.VMEM((8, 128), F32),
-        pltpu.VMEM((N, 1, W), F32),
+        pltpu.VMEM((N * 9, KC), BF16),
+        pltpu.VMEM((N * 9, W), F32),
+        pltpu.VMEM((N, 8, W + EXT), BF16),
+        pltpu.VMEM((N * 8, EXT), F32),
+        pltpu.VMEM((N, 8, W + EXT), BF16),
+        pltpu.VMEM((N, 128), I32),
+        pltpu.SMEM((N, 128), I32),
+        pltpu.VMEM((4 * N, 8, FZ), F32),
+        pltpu.VMEM((4 * N, FZ), F32),
+        pltpu.VMEM((DR * FX * FY, FZ), F32),
+        pltpu.VMEM((DR * 4 * N, FZ), F32),
         pltpu.VMEM((FX + 2, FY + 2, 16, FZ), F32),
         pltpu.VMEM((FX, FY * 8, FZ), F32),
-        pltpu.VMEM((HIGH * 8, W), BF16),
         pltpu.VMEM((N, 8, W), BF16),
         pltpu.VMEM((N, 8, W), BF16),
         pltpu.VMEM((N * 8, W), BF16),
-        dma((4,)), dma((4,)), dma((NSB,)), dma((NSB,)), dma((NSB,)), dma((NSB,)),
-        dma((8,)), dma((8,)), dma((NSB,)), dma((NSB,)),
+        dma((4,)), dma((4,)), dma((NSB,)), dma((NSB,)),
+        dma((8,)), dma((8,)), dma((NSB,)), dma((NSB,)), dma((NSB,)),
     ]
     return pl.pallas_call(
         body,

time: 86.4 us -> 74.1 us (0.86)
  Pallas kernels: 82.3 us -> 70 us
    pallas_call x1, Pallas kernels: 82.3 us -> 70 us  [per_device(): pl.pallas_call(body, out_shape=(jax.ShapeDtypeStruct((DR, FX, FY, FZ), BF...]
where the time goes in v1:
time: 74.1 us; the launch traced here: 73.9 us
  Pallas kernels  70 us (94%)
  local copies, waits for them, and re-layouts  3.29 us (4%)
    pallas_call x1, Pallas kernels, per_device(): pl.pallas_call(body, out_shape=(jax.ShapeDtypeStruct((DR, FX, FY, FZ), BF...  70 us
    unnamed x2, local copies, waits for them, and re-layouts  3.29 us

profile of v1, /device:TPU:1, one launch (start us, length us, event | category | flops | bytes accessed | tf_op | source)
XLA Modules:
  0.0 73.9 jit_solution(14794171803079293430)
XLA Ops:
  0.6 70.0 %shard_map.104 = (bf16[8,8,8,128]{3,2,1,0:T(8,128)(2,1)}, f32[8,10240]{1,0:T(8,128)}) custom-call(f32[16,8192]{1,0:T(8,128)} %part.1, s32[4,512]{1,0:T(4,128)} %midx.1, s32[1,4]{1,0:T(1,128)} %cnt.1, s32[80,128]{1,0:T(8,128)} %bitcast.3, s32[1,256]{1,0:T(1,128)} %size.1, s32[1,256]{1,0:T(1,128)} %bitcast.4, s32[1,256]{1,0:T(1,128)} %bitcast.5, ...), custom_call_target="tpu_custom_call" | custom-call | tf_op jit(solution)/shard_map/pallas_call | solution.py:457
  70.6 1.6 %copy.13 = bf16[8,8,8,128]{3,2,1,0:T(8,128)(2,1)} copy(bf16[8,8,8,128]{3,2,1,0:T(8,128)(2,1)} %get-tuple-element.4) | data formatting | bytes 262144
  72.2 1.7 %copy.14 = f32[8,10240]{1,0:T(8,128)} copy(f32[8,10240]{1,0:T(8,128)} %get-tuple-element.5) | data formatting | bytes 655360

commit v2 on v1

--- a/solution.py
+++ b/solution.py
@@ -25,12 +25,10 @@
 W = 256
 BLOCKS = SLOTS // W
 RES = PART // W
-RCH = 8
-LATE = 0
 PER = 4
 CHUNKS = BLOCKS // PER
 KC = PER * W
-ND = 32
+ND = 64
 NB = N // ND
 SB = 16
 NSB = N // SB
@@ -65,8 +63,8 @@
     part, midx, cnt, cell, size, owner, toff, clos, damp,
     drag_o, force_o,
     pt, smig, rmig, live, rel_a, rel_b, lall, m16s, den16s, abuf, acc,
-    sendm, ext, recvm, meta_v, meta_s, tiles, tden, flat, picked, gas, dtmp, sendr, retm, rbuf,
-    mig_ss, mig_rs, am_ss, am_rs, halo_ss, halo_rs, back_ss, back_rs, meta_sem,
+    sendm, ext, recvm, meta_v, meta_s, tiles, tden, flat, picked, keep8, gas, dtmp, sendr, retm, rbuf,
+    mig_ss, mig_rs, am_ss, am_rs, halo_ss, halo_rs, back_ss, back_rs, meta_sem, rows_sem,
 ):
     gx = lax.axis_index("gx")
     gy = lax.axis_index("gy")
@@ -81,9 +79,10 @@
 
     barrier = pltpu.get_barrier_semaphore()
 
-    @pl.loop(1, N)
-    def _(rel):
-        pl.semaphore_signal(barrier, 1, device_id=ahead(rel), device_id_type=MESH)
+    for k in range(1, N_GY):
+        pl.semaphore_signal(barrier, 1, device_id=beside(0, k), device_id_type=MESH)
+    for k in range(1, N_GX):
+        pl.semaphore_signal(barrier, 1, device_id=beside(k, 0), device_id_type=MESH)
 
     @pl.loop(0, RES)
     def _(g):
@@ -109,7 +108,7 @@
         hits = hits + dot_nt(high_hot, low_hot)
     live[0:RES] = 1.0 - hits
 
-    pl.semaphore_wait(barrier, N - 1)
+    pl.semaphore_wait(barrier, N_GX + N_GY - 2)
     mig = []
     for j, (dx, dy) in enumerate(((1, 0), (-1, 0), (0, 1), (0, -1))):
         copy = pltpu.make_async_remote_copy(
@@ -118,6 +117,8 @@
         )
         copy.start()
         mig.append(copy)
+    for k in range(1, N_GX):
+        pl.semaphore_signal(rows_sem, 1, device_id=beside(k, 0), device_id_type=MESH)
 
     sub = iota((TILES, TILES), 0)
     lane = iota((TILES, TILES), 1)
@@ -155,7 +156,7 @@
 
     sub16 = iota((16, W), 0)
 
-    def prepare(g, dep):
+    def prepare(g, dep, state):
         row = jnp.concatenate([cell[pl.ds(2 * g, 1), :], cell[pl.ds(2 * g + 1, 1), :]], axis=1)
         row = row.astype(F32)
         inside = jnp.where(start_col <= row, 1.0, 0.0).astype(BF16)
@@ -166,6 +167,7 @@
         lall[lax.div(g, PER), :, pl.ds(pl.multiple_of(lax.rem(g, PER) * W, W), W)] = hot
         rel_a[g] = (rel - jnp.where(sub16 >= 8, 1.0, 0.0)).astype(BF16)
         rel_b[g] = (rel - sub16.astype(F32)).astype(BF16)
+        keep8[g] = state
         mixed = dot_nn(clos2, dep)
         mixed = mixed[0:8] + mixed[8:16]
         m16s[g] = jnp.concatenate([mixed, mixed], axis=0).astype(BF16)
@@ -174,7 +176,17 @@
     @pl.loop(0, RES)
     def _(g):
         lanes = pl.ds(pl.multiple_of(g * W, W), W)
-        prepare(g, (part[:, lanes] * live[pl.ds(g, 1), :]).astype(BF16))
+        state = part[:, lanes]
+        prepare(g, (state * live[pl.ds(g, 1), :]).astype(BF16), state[0:8])
+
+    for copy in mig:
+        copy.wait_recv()
+    for j in range(4):
+        for h in range(2):
+            g = RES + 2 * j + h
+            live[g : g + 1] = rmig[j, CH : 2 * CH, h * W : (h + 1) * W].astype(F32)[0:1]
+            state = rmig[j, 0:CH, h * W : (h + 1) * W]
+            prepare(g, state, state.astype(F32)[0:8])
 
     zero16 = jnp.zeros((16, W), BF16)
 
@@ -193,24 +205,6 @@
                     near == float(first + 16 * k), den, zero16
                 )
 
-    def resident(c):
-        spread(c, 0, N, 0)
-        return dot_nt(abuf[...], lall[c])
-
-    acc[...] = jnp.zeros(acc.shape, F32)
-
-    @pl.loop(0, RCH - LATE)
-    def _(c):
-        acc[...] += resident(c)
-
-    for copy in mig:
-        copy.wait_recv()
-    for j in range(4):
-        for h in range(2):
-            g = RES + 2 * j + h
-            live[g : g + 1] = rmig[j, CH : 2 * CH, h * W : (h + 1) * W].astype(F32)[0:1]
-            prepare(g, rmig[j, 0:CH, h * W : (h + 1) * W])
-
     def send_out(rel):
         sb = lax.div(rel, SB)
         pltpu.make_async_remote_copy(
@@ -220,15 +214,15 @@
 
     for block in range(NB):
         rows = slice(block * ND * 8, (block + 1) * ND * 8)
-        drows = slice(N * 8 + block * ND, N * 8 + (block + 1) * ND)
-        mixed = acc[rows]
-        den = acc[drows]
-        for c in range(RCH, CHUNKS):
-            base = (c - RCH) * ND * 9
-            spread(c, block * ND, ND, base)
-            more = dot_nt(abuf[base : base + ND * 9], lall[c])
-            mixed = mixed + more[0 : ND * 8]
-            den = den + more[ND * 8 : ND * 9]
+        acc[...] = jnp.zeros(acc.shape, F32)
+
+        @pl.loop(0, CHUNKS)
+        def _(c):
+            spread(c, block * ND, ND, 0)
+            acc[...] += dot_nt(abuf[...], lall[c])
+
+        mixed = acc[0 : ND * 8]
+        den = acc[ND * 8 : ND * 9]
         sendm[block * ND : (block + 1) * ND, :, 0:W] = mixed.reshape(ND, 8, W).astype(BF16)
         den_hi = den.astype(BF16).astype(F32)
         den_lo = den - den_hi
@@ -244,6 +238,9 @@
         if block == 0:
             recvm[0] = sendm[0]
 
+        if block == 0:
+            pl.semaphore_wait(rows_sem, N_GX - 1)
+
         @pl.loop(1 if block == 0 else block * ND, (block + 1) * ND)
         def _(rel):
             send_out(rel)
@@ -253,6 +250,25 @@
 
     lane_row = iota((1, FZ), 1)
     first_half = lane_row < 64
+
+    def place(b):
+        wait_bytes(meta_s.at[pl.ds(b * SB, SB)], meta_sem.at[b])
+
+        @pl.loop(0, SB // UN)
+        def _(q):
+            for i in range(UN):
+                s = b * SB + q * UN + i
+                whole = recvm[s, :, 0:W].astype(F32)
+                for j in range(4):
+                    half = j // 2
+                    keep = first_half if j % 2 == 0 else ~first_half
+                    shift = (meta_s[s, j] + (0 if j % 2 == 0 else 64)) & (FZ - 1)
+                    at = slice(half * FZ, (half + 1) * FZ)
+                    tiles[j * N + s] = pltpu.roll(jnp.where(keep, whole[:, at], 0.0), shift, 1)
+                    den = ext[pl.ds(s * 8 + half, 1), :] + ext[pl.ds(s * 8 + 2 + half, 1), :]
+                    den = jnp.broadcast_to(jnp.where(keep, den, 0.0), (8, FZ))
+                    tden[pl.ds(j * N + s, 1), :] = pltpu.roll(den, shift, 1)[0:1]
+
     for b in range(NSB):
         wait_bytes(recvm.at[span(b)], am_rs.at[b])
         ext[b * SB * 8 : (b + 1) * SB * 8] = (
@@ -263,23 +279,9 @@
             meta_v.at[pl.ds(b * SB, SB)], meta_s.at[pl.ds(b * SB, SB)], meta_sem.at[b]
         ).start()
 
-    for b in range(NSB):
-        wait_bytes(meta_s.at[pl.ds(b * SB, SB)], meta_sem.at[b])
-
-    @pl.loop(0, N // UN)
-    def _(q):
-        for i in range(UN):
-            s = q * UN + i
-            whole = recvm[s, :, 0:W].astype(F32)
-            for j in range(4):
-                half = j // 2
-                keep = first_half if j % 2 == 0 else ~first_half
-                shift = (meta_s[s, j] + (0 if j % 2 == 0 else 64)) & (FZ - 1)
-                at = slice(half * FZ, (half + 1) * FZ)
-                tiles[j * N + s] = pltpu.roll(jnp.where(keep, whole[:, at], 0.0), shift, 1)
-                den = ext[pl.ds(s * 8 + half, 1), :] + ext[pl.ds(s * 8 + 2 + half, 1), :]
-                den = jnp.broadcast_to(jnp.where(keep, den, 0.0), (8, FZ))
-                tden[pl.ds(j * N + s, 1), :] = pltpu.roll(den, shift, 1)[0:1]
+        if b > 0:
+            place(b - 1)
+    place(NSB - 1)
 
     square = iota((N, N), 0) == iota((N, N), 1)
     meta_f = meta_v[...].astype(F32)
@@ -378,38 +380,40 @@
         for x in range(FX):
             drag_o[r, x] = dtmp[x, pl.ds(r, FY, stride=8), :].astype(BF16)
 
-    for b in range(NSB):
-        wait_bytes(retm.at[span(b)], back_rs.at[b])
-        back = retm[b * SB : (b + 1) * SB].astype(F32).reshape(SB * 8, W)
-        rbuf[b * SB * 8 : (b + 1) * SB * 8] = back.astype(BF16)
-
     rows8 = iota((8, W), 0)
     slip = jnp.zeros((8, W), F32)
     for r in range(DR):
         slip = jnp.where(rows8 == r, damp[r], slip)
 
-    def finish(g, c, i, state):
+    def look(g, c, i, first):
         hot = lall[c, :, i * W : (i + 1) * W]
         rel = jnp.broadcast_to(rel_a[g].astype(F32)[0:1], (8, W))
-        got = jnp.zeros((8, W), F32)
-        for b in range(NSB):
+        at = pl.ds(pl.multiple_of(g * W, W), W)
+        got = jnp.zeros((8, W), F32) if first == 0 else force_o[:, at]
+        for b in range(first, first + NSB // 2):
             full = dot_nn(rbuf[b * SB * 8 : (b + 1) * SB * 8], hot)
             for d in range(SB):
                 got = jnp.where(rel == float(b * SB + d), full[d * 8 : (d + 1) * 8], got)
-        force_o[:, pl.ds(pl.multiple_of(g * W, W), W)] = live[pl.ds(g, 1), :] * (
-            got - slip * state
-        )
-
-    @pl.loop(0, RES // PER)
-    def _(c):
-        for i in range(PER):
-            g = c * PER + i
-            finish(g, c, i, part[0:8, pl.ds(pl.multiple_of(g * W, W), W)])
-
-    for j in range(4):
-        for h in range(2):
-            g = RES + 2 * j + h
-            finish(g, g // PER, g % PER, rmig[j, 0:CH, h * W : (h + 1) * W].astype(F32)[0:8])
+        return at, got
+
+    for first in (0, NSB // 2):
+        for b in range(first, first + NSB // 2):
+            wait_bytes(retm.at[span(b)], back_rs.at[b])
+            back = retm[b * SB : (b + 1) * SB].astype(F32).reshape(SB * 8, W)
+            rbuf[b * SB * 8 : (b + 1) * SB * 8] = back.astype(BF16)
+        if first == 0:
+            @pl.loop(0, CHUNKS)
+            def _(c):
+                for i in range(PER):
+                    at, got = look(c * PER + i, c, i, 0)
+                    force_o[:, at] = got
+        else:
+            @pl.loop(0, CHUNKS)
+            def _(c):
+                for i in range(PER):
+                    g = c * PER + i
+                    at, got = look(g, c, i, first)
+                    force_o[:, at] = live[pl.ds(g, 1), :] * (got - slip * keep8[g])
 
     for copy in mig + halo:
         copy.wait_send()
@@ -435,8 +439,8 @@
         pltpu.VMEM((CHUNKS, W, KC), BF16),
         pltpu.VMEM((BLOCKS, 16, W), BF16),
         pltpu.VMEM((BLOCKS, 16, W), BF16),
-        pltpu.VMEM((N * 9, KC), BF16),
-        pltpu.VMEM((N * 9, W), F32),
+        pltpu.VMEM((ND * 9, KC), BF16),
+        pltpu.VMEM((ND * 9, W), F32),
         pltpu.VMEM((N, 8, W + EXT), BF16),
         pltpu.VMEM((N * 8, EXT), F32),
         pltpu.VMEM((N, 8, W + EXT), BF16),
@@ -446,13 +450,14 @@
         pltpu.VMEM((4 * N, FZ), F32),
         pltpu.VMEM((DR * FX * FY, FZ), F32),
         pltpu.VMEM((DR * 4 * N, FZ), F32),
+        pltpu.VMEM((BLOCKS, 8, W), F32),
         pltpu.VMEM((FX + 2, FY + 2, 16, FZ), F32),
         pltpu.VMEM((FX, FY * 8, FZ), F32),
         pltpu.VMEM((N, 8, W), BF16),
         pltpu.VMEM((N, 8, W), BF16),
         pltpu.VMEM((N * 8, W), BF16),
         dma((4,)), dma((4,)), dma((NSB,)), dma((NSB,)),
-        dma((8,)), dma((8,)), dma((NSB,)), dma((NSB,)), dma((NSB,)),
+        dma((8,)), dma((8,)), dma((NSB,)), dma((NSB,)), dma((NSB,)), pltpu.SemaphoreType.REGULAR,
     ]
     return pl.pallas_call(
         body,

time: 74.1 us -> 67 us (0.904)
  Pallas kernels: 70 us -> 62.9 us
    pallas_call x1, Pallas kernels: 70 us -> 62.9 us  [per_device(): pl.pallas_call(body, out_shape=(jax.ShapeDtypeStruct((DR, FX, FY, FZ), BF...]
where the time goes in v2:
time: 67 us; the launch traced here: 66.8 us
  Pallas kernels  62.9 us (94%)
  local copies, waits for them, and re-layouts  3.29 us (5%)
    pallas_call x1, Pallas kernels, per_device(): pl.pallas_call(body, out_shape=(jax.ShapeDtypeStruct((DR, FX, FY, FZ), BF...  62.9 us
    unnamed x2, local copies, waits for them, and re-layouts  3.29 us

profile of v2, /device:TPU:1, one launch (start us, length us, event | category | flops | bytes accessed | tf_op | source)
XLA Modules:
  0.0 66.8 jit_solution(5248939468761364912)
XLA Ops:
  0.6 62.9 %shard_map.104 = (bf16[8,8,8,128]{3,2,1,0:T(8,128)(2,1)}, f32[8,10240]{1,0:T(8,128)}) custom-call(f32[16,8192]{1,0:T(8,128)} %part.1, s32[4,512]{1,0:T(4,128)} %midx.1, s32[1,4]{1,0:T(1,128)} %cnt.1, s32[80,128]{1,0:T(8,128)} %bitcast.3, s32[1,256]{1,0:T(1,128)} %size.1, s32[1,256]{1,0:T(1,128)} %bitcast.4, s32[1,256]{1,0:T(1,128)} %bitcast.5, ...), custom_call_target="tpu_custom_call" | custom-call | tf_op jit(solution)/shard_map/pallas_call | solution.py:462
  63.6 1.6 %copy.13 = bf16[8,8,8,128]{3,2,1,0:T(8,128)(2,1)} copy(bf16[8,8,8,128]{3,2,1,0:T(8,128)(2,1)} %get-tuple-element.4) | data formatting | bytes 262144
  65.1 1.7 %copy.14 = f32[8,10240]{1,0:T(8,128)} copy(f32[8,10240]{1,0:T(8,128)} %get-tuple-element.5) | data formatting | bytes 655360

commit v3 on v2

--- a/solution.py
+++ b/solution.py
@@ -32,9 +32,10 @@
 NB = N // ND
 SB = 16
 NSB = N // SB
-UN = 4
-HOP = 37
-BACK = 45
+GROUPS = 96
+UN = 8
+HOP = 21
+BACK = 61
 EXT = 128
 SIDES = tuple((dx, dy) for dx in (-1, 0, 1) for dy in (-1, 0, 1) if dx or dy)
 
@@ -63,8 +64,8 @@
     part, midx, cnt, cell, size, owner, toff, clos, damp,
     drag_o, force_o,
     pt, smig, rmig, live, rel_a, rel_b, lall, m16s, den16s, abuf, acc,
-    sendm, ext, recvm, meta_v, meta_s, tiles, tden, flat, picked, keep8, gas, dtmp, sendr, retm, rbuf,
-    mig_ss, mig_rs, am_ss, am_rs, halo_ss, halo_rs, back_ss, back_rs, meta_sem, rows_sem,
+    sendm, ext, recvm, meta_v, meta_s, tiles, tden, flat, picked, cellv, own_v, own_s, keep8, gas, dtmp, sendr, retm, rbuf,
+    mig_ss, mig_rs, am_ss, am_rs, halo_ss, halo_rs, back_ss, back_rs, meta_sem, rows_sem, own_sem,
 ):
     gx = lax.axis_index("gx")
     gy = lax.axis_index("gy")
@@ -142,10 +143,19 @@
     off_high = (offs >> 7).astype(F32)
     sub128 = iota((N, TILES), 0)
     rank_of = (sub128 & 3).astype(F32)
+    start_int = start_row.astype(I32)
+    within = (start_int & 127).astype(F32)
+    group = (start_int >> 7).astype(F32)
     what = jnp.where(sub128 < 4, off_low, jnp.where(sub128 < 8, off_high, 0.0))
+    what = jnp.where((sub128 >= 8) & (sub128 < 12), within, what)
+    what = jnp.where((sub128 >= 12) & (sub128 < 16), group, what)
+    what = jnp.where((sub128 >= 16) & (sub128 < 20), size_row, what)
     what = jnp.where(rank_row == rank_of, what, 0.0).astype(BF16)
     rel_hot = jnp.where(sub128.astype(F32) == rel_row, 1.0, 0.0).astype(BF16)
     meta = dot_nt(rel_hot, what)
+    own_v[...] = meta.astype(I32)
+    own_copy = pltpu.make_async_copy(own_v, own_s, own_sem)
+    own_copy.start()
     for d in range(0, N, 8):
         ext[pl.ds(d * 8 + 4, 8, stride=8), :] = meta[d : d + 8]
 
@@ -385,35 +395,89 @@
     for r in range(DR):
         slip = jnp.where(rows8 == r, damp[r], slip)
 
-    def look(g, c, i, first):
-        hot = lall[c, :, i * W : (i + 1) * W]
-        rel = jnp.broadcast_to(rel_a[g].astype(F32)[0:1], (8, W))
-        at = pl.ds(pl.multiple_of(g * W, W), W)
-        got = jnp.zeros((8, W), F32) if first == 0 else force_o[:, at]
-        for b in range(first, first + NSB // 2):
-            full = dot_nn(rbuf[b * SB * 8 : (b + 1) * SB * 8], hot)
-            for d in range(SB):
-                got = jnp.where(rel == float(b * SB + d), full[d * 8 : (d + 1) * 8], got)
-        return at, got
-
-    for first in (0, NSB // 2):
-        for b in range(first, first + NSB // 2):
-            wait_bytes(retm.at[span(b)], back_rs.at[b])
-            back = retm[b * SB : (b + 1) * SB].astype(F32).reshape(SB * 8, W)
-            rbuf[b * SB * 8 : (b + 1) * SB * 8] = back.astype(BF16)
-        if first == 0:
-            @pl.loop(0, CHUNKS)
-            def _(c):
-                for i in range(PER):
-                    at, got = look(c * PER + i, c, i, 0)
-                    force_o[:, at] = got
-        else:
-            @pl.loop(0, CHUNKS)
-            def _(c):
-                for i in range(PER):
-                    g = c * PER + i
-                    at, got = look(g, c, i, first)
-                    force_o[:, at] = live[pl.ds(g, 1), :] * (got - slip * keep8[g])
+    own_copy.wait()
+    lanes = iota((8, FZ), 1)
+    own_f = own_v[...].astype(F32)
+    group_row = jnp.concatenate(
+        [
+            jnp.sum(jnp.where(square, own_f[:, 12 + j : 13 + j], 0.0), axis=0, keepdims=True)
+            for j in range(4)
+        ],
+        axis=1,
+    )
+    group_ids = iota((GROUPS, 4 * N), 0).astype(F32)
+    group_hot = jnp.concatenate(
+        [
+            jnp.where(group_ids == group_row, 1.0, 0.0),
+            jnp.where(group_ids == group_row + 1.0, 1.0, 0.0),
+        ],
+        axis=1,
+    ).astype(BF16)
+    begins = jnp.concatenate([own_f[:, 8 + j : 9 + j] for j in range(4)], axis=0)
+    here = jnp.where(iota((4 * N, FZ), 1).astype(F32) >= begins, 1.0, 0.0).astype(BF16)
+    after = (1.0 - here.astype(F32)).astype(BF16)
+
+    @pl.loop(0, CHUNKS)
+    def _(c):
+        for i in range(PER):
+            g = c * PER + i
+            row = jnp.concatenate([cell[pl.ds(2 * g, 1), :], cell[pl.ds(2 * g + 1, 1), :]], axis=1)
+            lall[c, :, i * W : (i + 1) * W] = jnp.where(
+                iota((W, W), 0) == (row & (W - 1)), 1.0, 0.0
+            ).astype(BF16)
+
+    for b in range(NSB):
+        wait_bytes(retm.at[span(b)], back_rs.at[b])
+
+        @pl.loop(0, SB // UN)
+        def _(q):
+            for i in range(UN):
+                s = b * SB + q * UN + i
+                whole = retm[s].astype(F32)
+                for j in range(4):
+                    half, base = j // 2, 64 * (j % 2)
+                    count = own_s[s, 16 + j]
+                    keep = (lanes >= base) & (lanes < base + count)
+                    value = jnp.where(keep, whole[:, half * FZ : (half + 1) * FZ], 0.0)
+                    shift = (own_s[s, 8 + j] - base) & (FZ - 1)
+                    tiles[j * N + s] = pltpu.roll(value, shift, 1)
+
+    for r in range(0, DR, 2):
+        pair = []
+        for k in range(2):
+            rows = tiles2(tiles, r + k)
+            pair.append(jnp.concatenate([rows * here, rows * after], axis=0))
+        got = dot_nn(group_hot, jnp.concatenate(pair, axis=1))
+        cellv[r * GROUPS : (r + 1) * GROUPS] = got[:, 0:FZ]
+        cellv[(r + 1) * GROUPS : (r + 2) * GROUPS] = got[:, FZ : 2 * FZ]
+    for h in range(0, GROUPS // 2, 2):
+        both = []
+        for k in range(2):
+            first = 2 * (h + k)
+            both.append(
+                jnp.concatenate(
+                    [
+                        cellv[pl.ds(first, 8, stride=GROUPS), :],
+                        cellv[pl.ds(first + 1, 8, stride=GROUPS), :],
+                    ],
+                    axis=1,
+                )
+            )
+        rbuf[h * 8 : (h + 2) * 8] = jnp.concatenate(both, axis=0).astype(BF16)
+
+    @pl.loop(0, CHUNKS)
+    def _(c):
+        for i in range(PER):
+            g = c * PER + i
+            row = jnp.concatenate([cell[pl.ds(2 * g, 1), :], cell[pl.ds(2 * g + 1, 1), :]], axis=1)
+            high = jnp.broadcast_to(row >> 8, (8, W))
+            full = dot_nn(rbuf[...], lall[c, :, i * W : (i + 1) * W])
+            got = jnp.zeros((8, W), F32)
+            for h in range(GROUPS // 2):
+                got = jnp.where(high == h, full[h * 8 : (h + 1) * 8], got)
+            force_o[:, pl.ds(pl.multiple_of(g * W, W), W)] = live[pl.ds(g, 1), :] * (
+                got - slip * keep8[g]
+            )
 
     for copy in mig + halo:
         copy.wait_send()
@@ -450,14 +514,17 @@
         pltpu.VMEM((4 * N, FZ), F32),
         pltpu.VMEM((DR * FX * FY, FZ), F32),
         pltpu.VMEM((DR * 4 * N, FZ), F32),
+        pltpu.VMEM((DR * GROUPS, FZ), F32),
+        pltpu.VMEM((N, 128), I32),
+        pltpu.SMEM((N, 128), I32),
         pltpu.VMEM((BLOCKS, 8, W), F32),
         pltpu.VMEM((FX + 2, FY + 2, 16, FZ), F32),
         pltpu.VMEM((FX, FY * 8, FZ), F32),
         pltpu.VMEM((N, 8, W), BF16),
         pltpu.VMEM((N, 8, W), BF16),
-        pltpu.VMEM((N * 8, W), BF16),
+        pltpu.VMEM((GROUPS * 4, W), BF16),
         dma((4,)), dma((4,)), dma((NSB,)), dma((NSB,)),
-        dma((8,)), dma((8,)), dma((NSB,)), dma((NSB,)), dma((NSB,)), pltpu.SemaphoreType.REGULAR,
+        dma((8,)), dma((8,)), dma((NSB,)), dma((NSB,)), dma((NSB,)), pltpu.SemaphoreType.REGULAR, dma(()),
     ]
     return pl.pallas_call(
         body,

time: 67 us -> 64.8 us (0.967)
  Pallas kernels: 62.9 us -> 60.7 us
    pallas_call x1, Pallas kernels: 62.9 us -> 60.7 us  [per_device(): pl.pallas_call(body, out_shape=(jax.ShapeDtypeStruct((DR, FX, FY, FZ), BF...]
where the time goes in v3:
time: 64.8 us; the launch traced here: 64.6 us
  Pallas kernels  60.7 us (94%)
  local copies, waits for them, and re-layouts  3.29 us (5%)
    pallas_call x1, Pallas kernels, per_device(): pl.pallas_call(body, out_shape=(jax.ShapeDtypeStruct((DR, FX, FY, FZ), BF...  60.7 us
    unnamed x2, local copies, waits for them, and re-layouts  3.29 us

profile of v3, /device:TPU:1, one launch (start us, length us, event | category | flops | bytes accessed | tf_op | source)
XLA Modules:
  0.0 64.6 jit_solution(8987792565921010158)
XLA Ops:
  0.6 60.7 %shard_map.104 = (bf16[8,8,8,128]{3,2,1,0:T(8,128)(2,1)}, f32[8,10240]{1,0:T(8,128)}) custom-call(f32[16,8192]{1,0:T(8,128)} %part.1, s32[4,512]{1,0:T(4,128)} %midx.1, s32[1,4]{1,0:T(1,128)} %cnt.1, s32[80,128]{1,0:T(8,128)} %bitcast.3, s32[1,256]{1,0:T(1,128)} %size.1, s32[1,256]{1,0:T(1,128)} %bitcast.4, s32[1,256]{1,0:T(1,128)} %bitcast.5, ...), custom_call_target="tpu_custom_call" | custom-call | tf_op jit(solution)/shard_map/pallas_call | solution.py:529
  61.3 1.6 %copy.13 = bf16[8,8,8,128]{3,2,1,0:T(8,128)(2,1)} copy(bf16[8,8,8,128]{3,2,1,0:T(8,128)(2,1)} %get-tuple-element.4) | data formatting | bytes 262144
  62.9 1.7 %copy.14 = f32[8,10240]{1,0:T(8,128)} copy(f32[8,10240]{1,0:T(8,128)} %get-tuple-element.5) | data formatting | bytes 655360

commit v4 on v3

--- a/solution.py
+++ b/solution.py
@@ -28,8 +28,6 @@
 PER = 4
 CHUNKS = BLOCKS // PER
 KC = PER * W
-ND = 64
-NB = N // ND
 SB = 16
 NSB = N // SB
 GROUPS = 96
@@ -125,19 +123,12 @@
     lane = iota((TILES, TILES), 1)
     size_row = size[...].astype(F32)
     own_row = owner[...].astype(F32)
-    start_col = jnp.sum(jnp.where(lane < sub, size_row, 0.0), axis=1, keepdims=True)
     size_col = jnp.sum(jnp.where(lane == sub, size_row, 0.0), axis=1, keepdims=True)
     start_row = jnp.sum(jnp.where(sub < lane, size_col, 0.0), axis=0, keepdims=True)
     own_col = jnp.sum(jnp.where(lane == sub, own_row, 0.0), axis=1, keepdims=True)
     earlier = jnp.where(own_col == own_row, jnp.where(sub < lane, 1.0, 0.0), 0.0)
     rank_row = jnp.sum(earlier, axis=0, keepdims=True)
     rel_row = (((owner[...] - me) * BACK) & (N - 1)).astype(F32)
-    base_row = 64.0 * rank_row - start_row
-    sub8 = iota((8, TILES), 0)
-    values = jnp.where(sub8 == 0, rel_row, jnp.where(sub8 == 1, base_row, 0.0))
-    before = jnp.where(iota((8, TILES), 1) == 0, 0.0, pltpu.roll(values, 1, 1))
-    steps = (values - before).astype(BF16)
-
     offs = toff[...]
     off_low = (offs & (FZ - 1)).astype(F32)
     off_high = (offs >> 7).astype(F32)
@@ -156,9 +147,6 @@
     own_v[...] = meta.astype(I32)
     own_copy = pltpu.make_async_copy(own_v, own_s, own_sem)
     own_copy.start()
-    for d in range(0, N, 8):
-        ext[pl.ds(d * 8 + 4, 8, stride=8), :] = meta[d : d + 8]
-
     clos_f = clos[...]
     clos_hi = clos_f.astype(BF16)
     clos_lo = (clos_f - clos_hi.astype(F32)).astype(BF16)
@@ -168,15 +156,11 @@
 
     def prepare(g, dep, state):
         row = jnp.concatenate([cell[pl.ds(2 * g, 1), :], cell[pl.ds(2 * g + 1, 1), :]], axis=1)
-        row = row.astype(F32)
-        inside = jnp.where(start_col <= row, 1.0, 0.0).astype(BF16)
-        found = dot_nn(steps, inside)
-        rel = found[0:1]
-        place = row + found[1:2]
-        hot = jnp.where(iota((W, W), 0).astype(F32) == place, 1.0, 0.0).astype(BF16)
+        hot = jnp.where(iota((W, W), 0) == (row & (W - 1)), 1.0, 0.0).astype(BF16)
         lall[lax.div(g, PER), :, pl.ds(pl.multiple_of(lax.rem(g, PER) * W, W), W)] = hot
-        rel_a[g] = (rel - jnp.where(sub16 >= 8, 1.0, 0.0)).astype(BF16)
-        rel_b[g] = (rel - sub16.astype(F32)).astype(BF16)
+        near = (row >> 8) - jnp.zeros((16, W), I32)
+        rel_a[g] = (near - jnp.where(sub16 >= 8, 1, 0)).astype(F32).astype(BF16)
+        rel_b[g] = (near - sub16).astype(F32).astype(BF16)
         keep8[g] = state
         mixed = dot_nn(clos2, dep)
         mixed = mixed[0:8] + mixed[8:16]
@@ -188,15 +172,6 @@
         lanes = pl.ds(pl.multiple_of(g * W, W), W)
         state = part[:, lanes]
         prepare(g, (state * live[pl.ds(g, 1), :]).astype(BF16), state[0:8])
-
-    for copy in mig:
-        copy.wait_recv()
-    for j in range(4):
-        for h in range(2):
-            g = RES + 2 * j + h
-            live[g : g + 1] = rmig[j, CH : 2 * CH, h * W : (h + 1) * W].astype(F32)[0:1]
-            state = rmig[j, 0:CH, h * W : (h + 1) * W]
-            prepare(g, state, state.astype(F32)[0:8])
 
     zero16 = jnp.zeros((16, W), BF16)
 
@@ -222,36 +197,112 @@
             device_id=ahead(rel), device_id_type=MESH,
         ).start()
 
-    for block in range(NB):
-        rows = slice(block * ND * 8, (block + 1) * ND * 8)
-        acc[...] = jnp.zeros(acc.shape, F32)
-
-        @pl.loop(0, CHUNKS)
-        def _(c):
-            spread(c, block * ND, ND, 0)
-            acc[...] += dot_nt(abuf[...], lall[c])
-
-        mixed = acc[0 : ND * 8]
-        den = acc[ND * 8 : ND * 9]
-        sendm[block * ND : (block + 1) * ND, :, 0:W] = mixed.reshape(ND, 8, W).astype(BF16)
-        den_hi = den.astype(BF16).astype(F32)
-        den_lo = den - den_hi
-        for d in range(0, ND, 8):
-            row = (block * ND + d) * 8
-            for half in range(2):
-                at = slice(half * 128, (half + 1) * 128)
-                ext[pl.ds(row + half, 8, stride=8), :] = den_hi[d : d + 8, at]
-                ext[pl.ds(row + 2 + half, 8, stride=8), :] = den_lo[d : d + 8, at]
-        sendm[block * ND : (block + 1) * ND, :, W : W + EXT] = (
-            ext[rows].reshape(ND, 8, EXT).astype(BF16)
+    acc[...] = jnp.zeros(acc.shape, F32)
+
+    @pl.loop(0, RES // PER)
+    def _(c):
+        spread(c, 0, GROUPS // 2, 0)
+        more = dot_nt(abuf[...], lall[c])
+        acc[0] += more[:, 0:FZ]
+        acc[1] += more[:, FZ : 2 * FZ]
+
+    for copy in mig:
+        copy.wait_recv()
+    for j in range(4):
+        for h in range(2):
+            g = RES + 2 * j + h
+            live[g : g + 1] = rmig[j, CH : 2 * CH, h * W : (h + 1) * W].astype(F32)[0:1]
+            state = rmig[j, 0:CH, h * W : (h + 1) * W]
+            prepare(g, state, state.astype(F32)[0:8])
+
+    @pl.loop(RES // PER, CHUNKS)
+    def _(c):
+        spread(c, 0, GROUPS // 2, 0)
+        more = dot_nt(abuf[...], lall[c])
+        acc[0] += more[:, 0:FZ]
+        acc[1] += more[:, FZ : 2 * FZ]
+
+    own_copy.wait()
+    own_f = own_v[...].astype(F32)
+    begins = jnp.concatenate([own_f[:, 8 + j : 9 + j] for j in range(4)], axis=0)
+    here_f = jnp.where(iota((4 * N, FZ), 1).astype(F32) >= begins, 1.0, 0.0)
+
+    def group_cols(step):
+        hots = []
+        for j in range(4):
+            col = own_v[:, 12 + j : 13 + j] + step
+            col = (col & 1) * (GROUPS // 2) + (col >> 1)
+            hots.append(jnp.where(iota((N, GROUPS), 1) == col, 1.0, 0.0))
+        return jnp.concatenate(hots, axis=0)
+
+    hot_a, hot_b = group_cols(0), group_cols(1)
+    hot_a16, hot_b16 = hot_a.astype(BF16), hot_b.astype(BF16)
+
+    def cells_of(ref_row, stride):
+        return jnp.concatenate(
+            [acc_at(ref_row, stride, 0), acc_at(ref_row, stride, 1)], axis=0
         )
-        if block == 0:
+
+    def acc_at(first, stride, odd):
+        if stride == 1:
+            return acc[odd, first : first + GROUPS // 2]
+        return acc[odd, pl.ds(first, GROUPS // 2, stride=stride), :]
+
+    for r in range(0, DR, 2):
+        pair = jnp.concatenate([cells_of(r, 8), cells_of(r + 1, 8)], axis=1).astype(BF16)
+        low_part, high_part = dot_nn(hot_a16, pair), dot_nn(hot_b16, pair)
+        for k in range(2):
+            at = slice(k * FZ, (k + 1) * FZ)
+            picked[(r + k) * 4 * N : (r + k + 1) * 4 * N] = jnp.where(
+                here_f > 0.0, low_part[:, at], high_part[:, at]
+            )
+    den = cells_of(GROUPS * 4, 1)
+    den_hi = den.astype(BF16)
+    den_lo = (den - den_hi.astype(F32)).astype(BF16)
+    den2 = jnp.concatenate([den_hi.astype(F32), den_lo.astype(F32)], axis=1).astype(BF16)
+    low_part, high_part = dot_nn(hot_a16, den2), dot_nn(hot_b16, den2)
+    tden[...] = jnp.where(
+        here_f > 0.0,
+        low_part[:, 0:FZ] + low_part[:, FZ : 2 * FZ],
+        high_part[:, 0:FZ] + high_part[:, FZ : 2 * FZ],
+    )
+
+    pl.semaphore_wait(rows_sem, N_GX - 1)
+    slot_lanes = iota((8, FZ), 1)
+    slot_rows = iota((8, FZ), 0)
+    for b in range(NSB):
+        @pl.loop(0, SB // UN)
+        def _(q):
+            for i in range(UN):
+                s = b * SB + q * UN + i
+                halves, dens = [], []
+                for half in range(2):
+                    total = jnp.zeros((8, FZ), F32)
+                    dtotal = jnp.zeros((8, FZ), F32)
+                    for j in (2 * half, 2 * half + 1):
+                        base = 64 * (j % 2)
+                        count = own_s[s, 16 + j]
+                        shift = (base - own_s[s, 8 + j]) & (FZ - 1)
+                        keep = (slot_lanes >= base) & (slot_lanes < base + count)
+                        value = picked[pl.ds(j * N + s, 8, stride=4 * N), :]
+                        total = jnp.where(keep, pltpu.roll(value, shift, 1), total)
+                        dval = jnp.broadcast_to(tden[pl.ds(j * N + s, 1), :], (8, FZ))
+                        dtotal = jnp.where(keep, pltpu.roll(dval, shift, 1), dtotal)
+                    halves.append(total)
+                    dens.append(dtotal)
+                sendm[s, :, 0:W] = jnp.concatenate(halves, axis=1).astype(BF16)
+                value = jnp.where((slot_rows & 1) == 0, dens[0], dens[1])
+                top = value.astype(BF16).astype(F32)
+                note = jnp.broadcast_to(own_v[pl.ds(s, 1), :].astype(F32), (8, FZ))
+                extra = jnp.where(
+                    slot_rows < 2, top, jnp.where(slot_rows < 4, value - top, note)
+                )
+                sendm[s, :, W : W + EXT] = extra.astype(BF16)
+
+        if b == 0:
             recvm[0] = sendm[0]
 
-        if block == 0:
-            pl.semaphore_wait(rows_sem, N_GX - 1)
-
-        @pl.loop(1 if block == 0 else block * ND, (block + 1) * ND)
+        @pl.loop(1 if b == 0 else b * SB, (b + 1) * SB)
         def _(rel):
             send_out(rel)
 
@@ -395,9 +446,7 @@
     for r in range(DR):
         slip = jnp.where(rows8 == r, damp[r], slip)
 
-    own_copy.wait()
     lanes = iota((8, FZ), 1)
-    own_f = own_v[...].astype(F32)
     group_row = jnp.concatenate(
         [
             jnp.sum(jnp.where(square, own_f[:, 12 + j : 13 + j], 0.0), axis=0, keepdims=True)
@@ -413,18 +462,8 @@
         ],
         axis=1,
     ).astype(BF16)
-    begins = jnp.concatenate([own_f[:, 8 + j : 9 + j] for j in range(4)], axis=0)
-    here = jnp.where(iota((4 * N, FZ), 1).astype(F32) >= begins, 1.0, 0.0).astype(BF16)
+    here = here_f.astype(BF16)
     after = (1.0 - here.astype(F32)).astype(BF16)
-
-    @pl.loop(0, CHUNKS)
-    def _(c):
-        for i in range(PER):
-            g = c * PER + i
-            row = jnp.concatenate([cell[pl.ds(2 * g, 1), :], cell[pl.ds(2 * g + 1, 1), :]], axis=1)
-            lall[c, :, i * W : (i + 1) * W] = jnp.where(
-                iota((W, W), 0) == (row & (W - 1)), 1.0, 0.0
-            ).astype(BF16)
 
     for b in range(NSB):
         wait_bytes(retm.at[span(b)], back_rs.at[b])
@@ -503,8 +542,8 @@
         pltpu.VMEM((CHUNKS, W, KC), BF16),
         pltpu.VMEM((BLOCKS, 16, W), BF16),
         pltpu.VMEM((BLOCKS, 16, W), BF16),
-        pltpu.VMEM((ND * 9, KC), BF16),
-        pltpu.VMEM((ND * 9, W), F32),
+        pltpu.VMEM((GROUPS // 2 * 9, KC), BF16),
+        pltpu.VMEM((2, GROUPS // 2 * 9, FZ), F32),
         pltpu.VMEM((N, 8, W + EXT), BF16),
         pltpu.VMEM((N * 8, EXT), F32),
         pltpu.VMEM((N, 8, W + EXT), BF16),

time: 64.8 us -> 62.4 us (0.963)
  Pallas kernels: 60.7 us -> 58.3 us
    pallas_call x1, Pallas kernels: 60.7 us -> 58.3 us  [per_device(): pl.pallas_call(body, out_shape=(jax.ShapeDtypeStruct((DR, FX, FY, FZ), BF...]
where the time goes in v4:
time: 62.4 us; the launch traced here: 62.2 us
  Pallas kernels  58.3 us (93%)
  local copies, waits for them, and re-layouts  3.29 us (5%)
  between operations  0.64 us (1%)
    pallas_call x1, Pallas kernels, per_device(): pl.pallas_call(body, out_shape=(jax.ShapeDtypeStruct((DR, FX, FY, FZ), BF...  58.3 us
    unnamed x2, local copies, waits for them, and re-layouts  3.29 us

profile of v4, /device:TPU:1, one launch (start us, length us, event | category | flops | bytes accessed | tf_op | source)
XLA Modules:
  0.0 62.2 jit_solution(13162201302247803643)
XLA Ops:
  0.6 58.3 %shard_map.104 = (bf16[8,8,8,128]{3,2,1,0:T(8,128)(2,1)}, f32[8,10240]{1,0:T(8,128)}) custom-call(f32[16,8192]{1,0:T(8,128)} %part.1, s32[4,512]{1,0:T(4,128)} %midx.1, s32[1,4]{1,0:T(1,128)} %cnt.1, s32[80,128]{1,0:T(8,128)} %bitcast.3, s32[1,256]{1,0:T(1,128)} %size.1, s32[1,256]{1,0:T(1,128)} %bitcast.4, s32[1,256]{1,0:T(1,128)} %bitcast.5, ...), custom_call_target="tpu_custom_call" | custom-call | tf_op jit(solution)/shard_map/pallas_call | solution.py:568
  59.0 1.6 %copy.13 = bf16[8,8,8,128]{3,2,1,0:T(8,128)(2,1)} copy(bf16[8,8,8,128]{3,2,1,0:T(8,128)(2,1)} %get-tuple-element.4) | data formatting | bytes 262144
  60.5 1.7 %copy.14 = f32[8,10240]{1,0:T(8,128)} copy(f32[8,10240]{1,0:T(8,128)} %get-tuple-element.5) | data formatting | bytes 655360

commit v5 on v4

--- a/solution.py
+++ b/solution.py
@@ -25,13 +25,13 @@
 W = 256
 BLOCKS = SLOTS // W
 RES = PART // W
-PER = 4
+PER = 8
 CHUNKS = BLOCKS // PER
 KC = PER * W
 SB = 16
 NSB = N // SB
 GROUPS = 96
-UN = 8
+UN = 16
 HOP = 21
 BACK = 61
 EXT = 128
@@ -270,11 +270,11 @@
     pl.semaphore_wait(rows_sem, N_GX - 1)
     slot_lanes = iota((8, FZ), 1)
     slot_rows = iota((8, FZ), 0)
-    for b in range(NSB):
-        @pl.loop(0, SB // UN)
-        def _(q):
-            for i in range(UN):
-                s = b * SB + q * UN + i
+    @pl.loop(0, NSB)
+    def _(b):
+        for _i in range(1):
+            for i in range(SB):
+                s = b * SB + i
                 halves, dens = [], []
                 for half in range(2):
                     total = jnp.zeros((8, FZ), F32)
@@ -299,12 +299,13 @@
                 )
                 sendm[s, :, W : W + EXT] = extra.astype(BF16)
 
-        if b == 0:
+        @pl.when(b == 0)
+        def _():
             recvm[0] = sendm[0]
 
-        @pl.loop(1 if b == 0 else b * SB, (b + 1) * SB)
-        def _(rel):
-            send_out(rel)
+        @pl.loop(0, SB)
+        def _(k):
+            pl.when(b * SB + k > 0)(lambda: send_out(b * SB + k))
 
     def span(b):
         return pl.ds(1, SB - 1) if b == 0 else pl.ds(b * SB, SB)

time: 62.4 us -> 60.3 us (0.966)
  Pallas kernels: 58.3 us -> 56.2 us
    pallas_call x1, Pallas kernels: 58.3 us -> 56.2 us  [per_device(): pl.pallas_call(body, out_shape=(jax.ShapeDtypeStruct((DR, FX, FY, FZ), BF...]
where the time goes in v5:
time: 60.3 us; the launch traced here: 60.1 us
  Pallas kernels  56.2 us (93%)
  local copies, waits for them, and re-layouts  3.29 us (5%)
  between operations  0.64 us (1%)
    pallas_call x1, Pallas kernels, per_device(): pl.pallas_call(body, out_shape=(jax.ShapeDtypeStruct((DR, FX, FY, FZ), BF...  56.2 us
    unnamed x2, local copies, waits for them, and re-layouts  3.29 us

profile of v5, /device:TPU:1, one launch (start us, length us, event | category | flops | bytes accessed | tf_op | source)
XLA Modules:
  0.0 60.1 jit_solution(16423804607724118307)
XLA Ops:
  0.6 56.2 %shard_map.104 = (bf16[8,8,8,128]{3,2,1,0:T(8,128)(2,1)}, f32[8,10240]{1,0:T(8,128)}) custom-call(f32[16,8192]{1,0:T(8,128)} %part.1, s32[4,512]{1,0:T(4,128)} %midx.1, s32[1,4]{1,0:T(1,128)} %cnt.1, s32[80,128]{1,0:T(8,128)} %bitcast.3, s32[1,256]{1,0:T(1,128)} %size.1, s32[1,256]{1,0:T(1,128)} %bitcast.4, s32[1,256]{1,0:T(1,128)} %bitcast.5, ...), custom_call_target="tpu_custom_call" | custom-call | tf_op jit(solution)/shard_map/pallas_call | solution.py:569
  56.8 1.6 %copy.13 = bf16[8,8,8,128]{3,2,1,0:T(8,128)(2,1)} copy(bf16[8,8,8,128]{3,2,1,0:T(8,128)(2,1)} %get-tuple-element.4) | data formatting | bytes 262144
  58.4 1.7 %copy.14 = f32[8,10240]{1,0:T(8,128)} copy(f32[8,10240]{1,0:T(8,128)} %get-tuple-element.5) | data formatting | bytes 655360

commit v6 on v5

--- a/solution.py
+++ b/solution.py
@@ -62,7 +62,7 @@
     part, midx, cnt, cell, size, owner, toff, clos, damp,
     drag_o, force_o,
     pt, smig, rmig, live, rel_a, rel_b, lall, m16s, den16s, abuf, acc,
-    sendm, ext, recvm, meta_v, meta_s, tiles, tden, flat, picked, cellv, own_v, own_s, keep8, gas, dtmp, sendr, retm, rbuf,
+    sendm, ext, recvm, meta_v, meta_s, tiles, tden, flat, picked, cellv, own_v, own_s, keep8, gas, gden, dtmp, sendr, retm, rbuf,
     mig_ss, mig_rs, am_ss, am_rs, halo_ss, halo_rs, back_ss, back_rs, meta_sem, rows_sem, own_sem,
 ):
     gx = lax.axis_index("gx")
@@ -366,8 +366,8 @@
     for x in range(FX):
         for y in range(FY):
             c = x * FY + y
-            gas[x + 1, y + 1, 0:8] = flat[pl.ds(c, 8, stride=64), :]
-            gas[x + 1, y + 1, 8:16] = jnp.broadcast_to(den[c : c + 1], (8, FZ))
+            gas[x + 1, y + 1] = flat[pl.ds(c, 8, stride=64), :]
+            gden[x + 1, y + 1] = den[c : c + 1]
 
     def edge(step, far):
         if step == 0:
@@ -378,12 +378,15 @@
 
     halo = []
     for i, (dx, dy) in enumerate(SIDES):
-        copy = pltpu.make_async_remote_copy(
-            gas.at[edge(dx, False), edge(dy, False)], gas.at[edge(dx, True), edge(dy, True)],
-            halo_ss.at[i], halo_rs.at[i], device_id=beside(dx, dy), device_id_type=MESH,
-        )
-        copy.start()
-        halo.append(copy)
+        for k, block in enumerate((gas, gden)):
+            copy = pltpu.make_async_remote_copy(
+                block.at[edge(dx, False), edge(dy, False)],
+                block.at[edge(dx, True), edge(dy, True)],
+                halo_ss.at[2 * i + k], halo_rs.at[2 * i + k],
+                device_id=beside(dx, dy), device_id_type=MESH,
+            )
+            copy.start()
+            halo.append(copy)
     for copy in halo:
         copy.wait_recv()
 
@@ -392,10 +395,11 @@
         for odd in range(2):
             x = 2 * x2 + odd
             over_x = [gas[x, y] + 2.0 * gas[x + 1, y] + gas[x + 2, y] for y in range(FY + 2)]
+            den_x = [gden[x, y] + 2.0 * gden[x + 1, y] + gden[x + 2, y] for y in range(FY + 2)]
             for y in range(FY):
                 smooth = (over_x[y] + 2.0 * over_x[y + 1] + over_x[y + 2]) * (1.0 / 16.0)
-                dens = smooth[8:16]
-                drag = smooth[0:8] / (1.0 + dens * dens)
+                dens = (den_x[y] + 2.0 * den_x[y + 1] + den_x[y + 2]) * (1.0 / 16.0)
+                drag = smooth / (1.0 + dens * dens)
                 dtmp[x, y * 8 : (y + 1) * 8] = drag
 
     tile_hot = jnp.concatenate(
@@ -558,13 +562,14 @@
         pltpu.VMEM((N, 128), I32),
         pltpu.SMEM((N, 128), I32),
         pltpu.VMEM((BLOCKS, 8, W), F32),
-        pltpu.VMEM((FX + 2, FY + 2, 16, FZ), F32),
+        pltpu.VMEM((FX + 2, FY + 2, 8, FZ), F32),
+        pltpu.VMEM((FX + 2, FY + 2, 1, FZ), F32),
         pltpu.VMEM((FX, FY * 8, FZ), F32),
         pltpu.VMEM((N, 8, W), BF16),
         pltpu.VMEM((N, 8, W), BF16),
         pltpu.VMEM((GROUPS * 4, W), BF16),
         dma((4,)), dma((4,)), dma((NSB,)), dma((NSB,)),
-        dma((8,)), dma((8,)), dma((NSB,)), dma((NSB,)), dma((NSB,)), pltpu.SemaphoreType.REGULAR, dma(()),
+        dma((16,)), dma((16,)), dma((NSB,)), dma((NSB,)), dma((NSB,)), pltpu.SemaphoreType.REGULAR, dma(()),
     ]
     return pl.pallas_call(
         body,

time: 60.3 us -> 61 us (1.012)
  Pallas kernels: 56.2 us -> 56.9 us
    pallas_call x1, Pallas kernels: 56.2 us -> 56.9 us  [per_device(): pl.pallas_call(body, out_shape=(jax.ShapeDtypeStruct((DR, FX, FY, FZ), BF...]
where the time goes in v6:
time: 61 us; the launch traced here: 60.8 us
  Pallas kernels  56.9 us (93%)
  local copies, waits for them, and re-layouts  3.29 us (5%)
  between operations  0.64 us (1%)
    pallas_call x1, Pallas kernels, per_device(): pl.pallas_call(body, out_shape=(jax.ShapeDtypeStruct((DR, FX, FY, FZ), BF...  56.9 us
    unnamed x2, local copies, waits for them, and re-layouts  3.29 us

profile of v6, /device:TPU:1, one launch (start us, length us, event | category | flops | bytes accessed | tf_op | source)
XLA Modules:
  0.0 60.8 jit_solution(834541010187524916)
XLA Ops:
  0.6 56.9 %shard_map.104 = (bf16[8,8,8,128]{3,2,1,0:T(8,128)(2,1)}, f32[8,10240]{1,0:T(8,128)}) custom-call(f32[16,8192]{1,0:T(8,128)} %part.1, s32[4,512]{1,0:T(4,128)} %midx.1, s32[1,4]{1,0:T(1,128)} %cnt.1, s32[80,128]{1,0:T(8,128)} %bitcast.3, s32[1,256]{1,0:T(1,128)} %size.1, s32[1,256]{1,0:T(1,128)} %bitcast.4, s32[1,256]{1,0:T(1,128)} %bitcast.5, ...), custom_call_target="tpu_custom_call" | custom-call | tf_op jit(solution)/shard_map/pallas_call | solution.py:574
  57.5 1.6 %copy.13 = bf16[8,8,8,128]{3,2,1,0:T(8,128)(2,1)} copy(bf16[8,8,8,128]{3,2,1,0:T(8,128)(2,1)} %get-tuple-element.4) | data formatting | bytes 262144
  59.1 1.7 %copy.14 = f32[8,10240]{1,0:T(8,128)} copy(f32[8,10240]{1,0:T(8,128)} %get-tuple-element.5) | data formatting | bytes 655360
